TPU v7x, 128 devices: a whole 4x4x4 slice. The times are simulated.
128 devices in a mesh: gx: 4 (over x_lo, core), gy: 8 (over z, x_hi), gz: 4 (over y).
Axes of the slice: x: 4 (x_hi: 2, x_lo: 2; x = x_hi * 2 + x_lo), y: 4, z: 4, core: 2. Of those that a mesh axis runs over, the one named last changes fastest.
Arguments:
- load: float32 [3, 128, 256, 512], P(None, 'gz', 'gy', 'gx'), may hold values from -6 to 6
- labels: int32 [128, 256, 512], P('gz', 'gy', 'gx'), may hold values from 0 to 15
- mask: int32 [128, 256, 512], P('gz', 'gy', 'gx'), may hold values 0 or 1
- table: float32 [16], replicated, may hold values from 0.25 to 2
Outputs:
- displacement: float32 [3, 128, 256, 512], P(None, 'gz', 'gy', 'gx')
- residual: float32 [3, 128, 256, 512], P(None, 'gz', 'gy', 'gx')
All inputs are finite; a program needn't handle non-finite values. No bound on the sum of `mask` on one device may be relied on, other than what follows from the above.
Results may differ from a plain program's by a relative error of at most 0.0003.
Values sent between devices are 32-bit elements; how exact they have to be, the bound alone decides.
A program may use at most 128 MiB of HBM per device.

v0:
```python
import jax
import jax.numpy as jnp
from jax import lax
from jax.sharding import PartitionSpec as P

BRICK = 32
INTERSECTION = 4
SWEEPS = 2


LAMBDA_RATIO = 2.0
SIGMA_SHIFT = 0.1
REF_MODULUS = 1.5
VOID_MODULUS = 0.1
HIGHEST = lax.Precision.HIGHEST


def with_halo(cells, sides, width):
    for axis, dim in sides:
        count = lax.axis_size(axis)
        ends = count - 1
        head = lax.slice_in_dim(cells, 0, width, axis=dim)
        tail = lax.slice_in_dim(cells, cells.shape[dim] - width, cells.shape[dim], axis=dim)
        cells = jnp.concatenate(
            [
                lax.ppermute(tail, axis, [(i, (i + 1) % count) for i in range(ends)]),
                cells,
                lax.ppermute(head, axis, [((i + 1) % count, i) for i in range(ends)]),
            ],
            axis=dim,
        )
    return cells


def stiffness_ratio(component, direction):
    return LAMBDA_RATIO if component == direction else 1.0


def sine_table(length):
    grid = jnp.arange(1, length + 1, dtype=jnp.float32)
    return jnp.sqrt(2.0 / (length + 1)) * jnp.sin(
        jnp.pi * grid[:, None] * grid[None, :] / (length + 1)
    )


def eigen_values(length):
    grid = jnp.arange(1, length + 1, dtype=jnp.float32)
    return 2.0 - 2.0 * jnp.cos(jnp.pi * grid / (length + 1))


def ramp_weights(length, margin):
    position = jnp.arange(length, dtype=jnp.float32)
    rising = (position + 0.5) / (2 * margin)
    falling = (length - 0.5 - position) / (2 * margin)
    return jnp.minimum(jnp.minimum(rising, falling), 1.0)


def operator_core(padded_field, padded_modulus):
    centre_modulus = padded_modulus[1:-1, 1:-1, 1:-1]
    centre = padded_field[:, 1:-1, 1:-1, 1:-1]
    windows = []
    faces = []
    for direction in range(3):
        for offset in (0, 2):
            window = [slice(1, -1), slice(1, -1), slice(1, -1)]
            window[direction] = slice(offset, offset + centre_modulus.shape[direction])
            window = tuple(window)
            windows.append(window)
            faces.append(0.5 * (centre_modulus + padded_modulus[window]))
    results = []
    for component in range(3):
        total = SIGMA_SHIFT * centre_modulus * centre[component]
        for number in range(6):
            direction = number // 2
            total = total + stiffness_ratio(component, direction) * faces[number] * (
                centre[component] - padded_field[component][windows[number]]
            )
        results.append(total)
    return jnp.stack(results)


def transform_all(values, along_x, along_y, along_z):
    values = jnp.einsum("czyx,xk->czyk", values, along_x, precision=HIGHEST)
    values = jnp.einsum("czyx,yk->czkx", values, along_y, precision=HIGHEST)
    return jnp.einsum("czyx,zk->ckyx", values, along_z, precision=HIGHEST)


def fold_margin(values, dim, margin):
    extent = values.shape[dim]
    owned = extent - 4 * margin
    centre = lax.slice_in_dim(values, 2 * margin, 2 * margin + owned, axis=dim)
    lower = lax.slice_in_dim(values, 0, margin, axis=dim)
    upper = lax.slice_in_dim(values, extent - margin, extent, axis=dim)
    low_pad = [(0, 0)] * values.ndim
    low_pad[dim] = (0, owned - margin)
    high_pad = [(0, 0)] * values.ndim
    high_pad[dim] = (owned - margin, 0)
    return centre + jnp.pad(lower, low_pad) + jnp.pad(upper, high_pad)


def widen(residual):
    return with_halo(residual, (("gx", 3), ("gy", 2), ("gz", 1)), INTERSECTION)


def local(load, labels, mask, table):
    length = BRICK + 2 * INTERSECTION
    count_x = load.shape[3] // BRICK
    wide_x = count_x * BRICK + 2 * INTERSECTION
    sine = sine_table(length)
    eigen = eigen_values(length)
    eigen_wide = jnp.tile(eigen, count_x)
    denominators = jnp.stack(
        [
            REF_MODULUS
            * (
                stiffness_ratio(component, 0) * eigen[:, None, None]
                + stiffness_ratio(component, 1) * eigen[None, :, None]
                + stiffness_ratio(component, 2) * eigen_wide[None, None, :]
                + SIGMA_SHIFT
            )
            for component in range(3)
        ]
    )
    ramp = ramp_weights(length, INTERSECTION)
    ramped_sine = ramp[:, None] * sine
    position = jnp.arange(wide_x, dtype=jnp.int32)
    brick_start = jnp.arange(count_x, dtype=jnp.int32) * BRICK
    inner = jnp.arange(length, dtype=jnp.int32)
    picker = jnp.where(
        position[:, None, None] - brick_start[None, :, None] == inner[None, None, :], 1.0, 0.0
    )
    forward_x = jnp.einsum("xbi,ik->xbk", picker, ramped_sine, precision=HIGHEST).reshape(
        wide_x, count_x * length
    )
    backward_x = jnp.einsum("xbi,ki->bkx", picker, sine, precision=HIGHEST).reshape(
        count_x * length, wide_x
    )
    picks = jnp.arange(table.shape[0], dtype=jnp.int32)
    looked = jnp.sum(
        jnp.where(labels[None] == picks[:, None, None, None], table[:, None, None, None], 0.0),
        axis=0,
    )
    modulus = jnp.where(mask == 1, looked, VOID_MODULUS)
    solution = jnp.zeros_like(load)
    modulus_near = with_halo(modulus, (("gx", 2), ("gy", 1), ("gz", 0)), 1)
    residual = load
    for sweep in range(SWEEPS):
        spectrum = transform_all(widen(residual), forward_x, ramped_sine, ramped_sine)
        arrived = with_halo(
            transform_all(spectrum / denominators, backward_x, sine, sine),
            (("gx", 3), ("gy", 2), ("gz", 1)),
            INTERSECTION,
        )
        fold_arrived = arrived
        for dim in (1, 2, 3):
            fold_arrived = fold_margin(fold_arrived, dim, INTERSECTION)
        solution = solution + fold_arrived
        nearby = with_halo(fold_arrived, (("gx", 3), ("gy", 2), ("gz", 1)), 1)
        residual = residual - operator_core(nearby, modulus_near)
    return (solution, residual)


def solution(mesh):
    placed = (P(None, "gz", "gy", "gx"), P("gz", "gy", "gx"), P("gz", "gy", "gx"), P())
    return jax.shard_map(
        local,
        mesh=mesh,
        in_specs=placed,
        out_specs=(P(None, "gz", "gy", "gx"), P(None, "gz", "gy", "gx")),
        check_vma=False,
    )
```

profile of v0, /device:TPU:1, one launch (start us, length us, event | category | flops | bytes accessed | tf_op | source)
XLA Modules:
  0.0 452.3 jit_solution(1975219434514591336)
XLA Ops:
  28.3 6.8 %collective-permute-done.2 = f32[3,32,4,136]{3,1,2,0:T(8,128)S(1)} collective-permute-done((f32[3,32,4,136]{3,1,2,0:T(8,128)S(1)}, f32[3,32,4,136]{3,1,2,0:T(8,128)S(1)}, u32[]{:S(2)}, u32[]{:S(2)}) %collective-permute-start.2) | collective-permute-done | bytes 208928 | tf_op jit(solution)/shard_map/ppermute | solution.py:26
  35.3 10.2 %collective-permute-done.3 = f32[3,32,4,136]{3,1,2,0:T(8,128)S(1)} collective-permute-done((f32[3,32,4,136]{3,1,2,0:T(8,128)S(1)}, f32[3,32,4,136]{3,1,2,0:T(8,128)S(1)}, u32[]{:S(2)}, u32[]{:S(2)}) %collective-permute-start.3) | collective-permute-done | bytes 208928 | tf_op jit(solution)/shard_map/ppermute | solution.py:28
  51.5 8.8 %collective-permute-done.4 = f32[3,4,40,136]{3,2,1,0:T(8,128)S(1)} collective-permute-done((f32[3,4,40,136]{3,2,1,0:T(8,128)S(1)}, f32[3,4,40,136]{3,2,1,0:T(8,128)S(1)}, u32[]{:S(2)}, u32[]{:S(2)}) %collective-permute-start.4) | collective-permute-done | bytes 261152 | tf_op jit(solution)/shard_map/ppermute | solution.py:26
  64.2 5.0 %fusion = f32[3,40,40,160]{3,2,1,0:T(8,128)S(1)} fusion(f32[136,160,1,1]{0,1,3,2:T(8,128)S(1)} %bitcast.116, f32[3,4,40,136]{3,2,1,0:T(8,128)S(1)} %collective-permute-done.5, f32[3,32,4,136]{3,2,1,0:T(4,128)S(1)} %copy.92, f32[3,32,32,4]{3,2,1,0:T(8,128)S(1)} %copy-done.29, f32[3,32,32,128]{3,2,1,0:T(8,128)S(1)} %copy-done.4, ...), kind=kOutput, calls=%fused_computation.4 | convolution fusion | flops 1257292800 | bytes 5770240 | tf_op jit(solution)/shard_map/czyx,xk->czyk/dot_general | solution.py:83
  74.1 7.0 %bitcast_divide_fusion.1 = f32[3,40,40,160]{3,1,2,0:T(8,128)S(1)} fusion(f32[1,40,40,160]{3,1,2,0:T(8,128)S(1)} %add_multiply_fusion, f32[1,40,40,160]{3,1,2,0:T(8,128)S(1)} %copy-done.39, f32[1,40,40,160]{3,1,2,0:T(8,128)S(1)} %copy-done.37, f32[3,40,40,160]{3,2,1,0:T(8,128)S(1)} %convolution_bitcast_fusion.3, f32[40]{0:T(128)S(1)} %fusion.207, ...), kind=kOutput, calls=%fused_computation.21 | convolution fusion | flops 370948800 | bytes 9216480 | tf_op jit(solution)/shard_map/czyx,zk->ckyx/dot_general | solution.py:85
  81.2 5.3 %fusion.24 = f32[3,40,40,136]{3,2,1,0:T(8,128)S(1)} fusion(f32[160,136,1,1]{1,0,3,2:T(8,128)S(1)} %bitcast.114, f32[3,40,40,160]{3,1,2,0:T(8,128)S(1)} %bitcast_divide_fusion.1), kind=kOutput, calls=%fused_computation.32 | convolution fusion | flops 1253376000 | bytes 5770240 | tf_op jit(solution)/shard_map/czyx,xk->czyk/dot_general | solution.py:83
  86.5 5.0 %convolution_bitcast_fusion.2 = f32[3,40,40,136]{3,2,1,0:T(8,128)S(1)} fusion(f32[3,40,40,136]{3,2,1,0:T(8,128)S(1)} %fusion.24, f32[40]{0:T(128)S(1)} %get-tuple-element.70, f32[40]{0:T(128)S(1)} %get-tuple-element.71), kind=kOutput, calls=%fused_computation.52 | convolution fusion | flops 313348800 | bytes 5222720 | tf_op jit(solution)/shard_map/czyx,yk->czkx/dot_general | solution.py:84
  91.5 6.4 %fusion.34 = f32[3,40,40,136]{3,1,2,0:T(8,128)S(1)} fusion(f32[3,40,40,136]{3,2,1,0:T(8,128)S(1)} %convolution_bitcast_fusion.2, f32[40]{0:T(128)S(1)} %get-tuple-element.70, f32[40]{0:T(128)S(1)} %get-tuple-element.71), kind=kOutput, calls=%fused_computation.48 | convolution fusion | flops 313348800 | bytes 5222720 | tf_op jit(solution)/shard_map/czyx,zk->ckyx/dot_general | solution.py:85
  128.4 5.2 %collective-permute-done.8 = f32[3,40,4,144]{3,1,2,0:T(8,128)S(1)} collective-permute-done((f32[3,40,4,144]{3,1,2,0:T(8,128)S(1)}, f32[3,40,4,144]{3,1,2,0:T(8,128)S(1)}, u32[]{:S(2)}, u32[]{:S(2)}) %collective-permute-start.8) | collective-permute-done | bytes 276512 | tf_op jit(solution)/shard_map/ppermute | solution.py:26
  133.5 12.8 %collective-permute-done.9 = f32[3,40,4,144]{3,1,2,0:T(8,128)S(1)} collective-permute-done((f32[3,40,4,144]{3,1,2,0:T(8,128)S(1)}, f32[3,40,4,144]{3,1,2,0:T(8,128)S(1)}, u32[]{:S(2)}, u32[]{:S(2)}) %collective-permute-start.9) | collective-permute-done | bytes 276512 | tf_op jit(solution)/shard_map/ppermute | solution.py:28
  198.0 5.5 %collective-permute-start.14 = (f32[32,1,130]{2,0,1:T(8,128)S(1)}, f32[32,1,130]{2,0,1:T(8,128)S(1)}, u32[]{:S(2)}, u32[]{:S(2)}) collective-permute-start(f32[32,1,130]{2,0,1:T(8,128)S(1)} %get-tuple-element.58), channel_id=1, source_target_pairs={{0,4},{4,8},{8,12},{12,16},{16,20},{20,24},{24,28},{1,5},{5,9},{9,... | collective-permute-start | bytes 49928 | tf_op jit(solution)/shard_map/ppermute | solution.py:26
  231.3 5.7 %collective-permute-start.24 = (f32[3,32,32,4]{2,1,3,0:T(8,128)S(1)}, f32[3,32,32,4]{2,1,3,0:T(8,128)S(1)}, u32[]{:S(2)}, u32[]{:S(2)}) collective-permute-start(f32[3,32,32,4]{2,1,3,0:T(8,128)S(1)} %copy.110), channel_id=1, source_target_pairs={{0,32},{32,64},{64,96},{1,33},{33,65},{65,97},{2,34},{34,66},{66,9... | collective-permute-start | bytes 147464 | tf_op jit(solution)/shard_map/ppermute | solution.py:26
  251.5 6.5 %collective-permute-start.26 = (f32[3,32,4,136]{3,1,2,0:T(8,128)S(1)}, f32[3,32,4,136]{3,1,2,0:T(8,128)S(1)}, u32[]{:S(2)}, u32[]{:S(2)}) collective-permute-start(f32[3,32,4,136]{3,1,2,0:T(8,128)S(1)} %get-tuple-element.39), channel_id=1, source_target_pairs={{0,4},{4,8},{8,12},{12,16},{16,20},{20,24},{24,28},{1,5},{5,9},{9,... | collective-permute-start | bytes 626696 | tf_op jit(solution)/shard_map/ppermute | solution.py:26
  263.8 12.2 %collective-permute-done.27 = f32[3,32,4,136]{3,1,2,0:T(8,128)S(1)} collective-permute-done((f32[3,32,4,136]{3,1,2,0:T(8,128)S(1)}, f32[3,32,4,136]{3,1,2,0:T(8,128)S(1)}, u32[]{:S(2)}, u32[]{:S(2)}) %collective-permute-start.27) | collective-permute-done | bytes 208928 | tf_op jit(solution)/shard_map/ppermute | solution.py:28
  281.5 7.5 %collective-permute-done.28 = f32[3,4,40,136]{3,1,2,0:T(4,128)S(1)} collective-permute-done((f32[3,4,40,136]{3,1,2,0:T(4,128)S(1)}, f32[3,4,40,136]{3,1,2,0:T(4,128)S(1)}, u32[]{:S(2)}, u32[]{:S(2)}) %collective-permute-start.28) | collective-permute-done | bytes 261152 | tf_op jit(solution)/shard_map/ppermute | solution.py:26
  297.5 5.2 %fusion.20 = f32[3,40,40,160]{3,2,1,0:T(8,128)S(1)} fusion(f32[136,160,1,1]{0,1,3,2:T(8,128)S(1)} %bitcast.117, f32[3,40,40,136]{3,1,2,0:T(8,128)S(1)} %pad_maximum_fusion.3), kind=kOutput, calls=%fused_computation.28 | convolution fusion | flops 1253376000 | bytes 5770240 | tf_op jit(solution)/shard_map/czyx,xk->czyk/dot_general | solution.py:83
  307.7 7.0 %bitcast_divide_fusion = f32[3,40,40,160]{3,1,2,0:T(8,128)S(1)} fusion(f32[1,40,40,160]{3,1,2,0:T(8,128)S(1)} %copy-done.42, f32[1,40,40,160]{3,1,2,0:T(8,128)S(1)} %copy-done.40, f32[1,40,40,160]{3,1,2,0:T(8,128)S(1)} %copy-done.38, f32[3,40,40,160]{3,2,1,0:T(8,128)S(1)} %convolution_bitcast_fusion.1, f32[40]{0:T(128)S(1)} %fusion.207, ...), kind=kOutput, calls=%fused_computation.20 | convolution fusion | flops 370948800 | bytes 9216480 | tf_op jit(solution)/shard_map/czyx,zk->ckyx/dot_general | solution.py:85
  314.7 5.3 %fusion.16 = f32[3,40,40,136]{3,2,1,0:T(8,128)S(1)} fusion(f32[160,136,1,1]{1,0,3,2:T(8,128)S(1)} %bitcast.115, f32[3,40,40,160]{3,1,2,0:T(8,128)S(1)} %bitcast_divide_fusion), kind=kOutput, calls=%fused_computation.24 | convolution fusion | flops 1253376000 | bytes 5770240 | tf_op jit(solution)/shard_map/czyx,xk->czyk/dot_general | solution.py:83
  320.0 5.0 %convolution_bitcast_fusion = f32[3,40,40,136]{3,2,1,0:T(8,128)S(1)} fusion(f32[3,40,40,136]{3,2,1,0:T(8,128)S(1)} %fusion.16, f32[40]{0:T(128)S(1)} %get-tuple-element.70, f32[40]{0:T(128)S(1)} %get-tuple-element.71), kind=kOutput, calls=%fused_computation.50 | convolution fusion | flops 313348800 | bytes 5222720 | tf_op jit(solution)/shard_map/czyx,yk->czkx/dot_general | solution.py:84
  325.1 6.4 %fusion.37 = f32[3,40,40,136]{3,1,2,0:T(8,128)S(1)} fusion(f32[3,40,40,136]{3,2,1,0:T(8,128)S(1)} %convolution_bitcast_fusion, f32[40]{0:T(128)S(1)} %get-tuple-element.70, f32[40]{0:T(128)S(1)} %get-tuple-element.71), kind=kOutput, calls=%fused_computation.49 | convolution fusion | flops 313348800 | bytes 5222720 | tf_op jit(solution)/shard_map/czyx,zk->ckyx/dot_general | solution.py:85
  362.4 5.7 %collective-permute-done.32 = f32[3,40,4,144]{3,1,2,0:T(8,128)S(1)} collective-permute-done((f32[3,40,4,144]{3,1,2,0:T(8,128)S(1)}, f32[3,40,4,144]{3,1,2,0:T(8,128)S(1)}, u32[]{:S(2)}, u32[]{:S(2)}) %collective-permute-start.32) | collective-permute-done | bytes 276512 | tf_op jit(solution)/shard_map/ppermute | solution.py:26
  368.0 12.5 %collective-permute-done.33 = f32[3,40,4,144]{3,1,2,0:T(8,128)S(1)} collective-permute-done((f32[3,40,4,144]{3,1,2,0:T(8,128)S(1)}, f32[3,40,4,144]{3,1,2,0:T(8,128)S(1)}, u32[]{:S(2)}, u32[]{:S(2)}) %collective-permute-start.33) | collective-permute-done | bytes 276512 | tf_op jit(solution)/shard_map/ppermute | solution.py:28
  387.7 6.2 %collective-permute-done.34 = f32[3,4,48,144]{3,1,2,0:T(4,128)S(1)} collective-permute-done((f32[3,4,48,144]{3,1,2,0:T(4,128)S(1)}, f32[3,4,48,144]{3,1,2,0:T(4,128)S(1)}, u32[]{:S(2)}, u32[]{:S(2)}) %collective-permute-start.34) | collective-permute-done | bytes 331808 | tf_op jit(solution)/shard_map/ppermute | solution.py:26
  425.3 5.2 %collective-permute-done.39 = f32[3,32,1,130]{3,1,2,0:T(8,128)S(1)} collective-permute-done((f32[3,32,1,130]{3,1,2,0:T(8,128)S(1)}, f32[3,32,1,130]{3,1,2,0:T(8,128)S(1)}, u32[]{:S(2)}, u32[]{:S(2)}) %collective-permute-start.39) | collective-permute-done | bytes 49952 | tf_op jit(solution)/shard_map/ppermute | solution.py:28
  (273 shorter events, 281.4 us)
Async XLA Ops:
  4.6 11.3 %collective-permute-start = (f32[3,32,32,4]{2,1,3,0:T(8,128)}, f32[3,32,32,4]{2,1,3,0:T(8,128)}, u32[]{:S(2)}, u32[]{:S(2)}) collective-permute-start(f32[3,32,32,4]{2,1,3,0:T(8,128)} %copy.142), channel_id=1, source_target_pairs={{0,32},{32,64},{64,96},{1,33},{33,65},{65,97},{2,34},{34,66},{66,9... | collective-permute-start | bytes 147464 | tf_op jit(solution)/shard_map/ppermute | solution.py:26
  22.5 12.5 %collective-permute-start.2 = (f32[3,32,4,136]{3,1,2,0:T(8,128)S(1)}, f32[3,32,4,136]{3,1,2,0:T(8,128)S(1)}, u32[]{:S(2)}, u32[]{:S(2)}) collective-permute-start(f32[3,32,4,136]{3,1,2,0:T(8,128)S(1)} %copy.89), channel_id=1, source_target_pairs={{0,4},{4,8},{8,12},{12,16},{16,20},{20,24},{24,28},{1,5},{5,9},{9,... | collective-permute-start | bytes 626696 | tf_op jit(solution)/shard_map/ppermute | solution.py:26
  27.0 18.5 %collective-permute-start.3 = (f32[3,32,4,136]{3,1,2,0:T(8,128)S(1)}, f32[3,32,4,136]{3,1,2,0:T(8,128)S(1)}, u32[]{:S(2)}, u32[]{:S(2)}) collective-permute-start(f32[3,32,4,136]{3,1,2,0:T(8,128)S(1)} %copy.90), channel_id=1, source_target_pairs={{4,0},{8,4},{12,8},{16,12},{20,16},{24,20},{28,24},{5,1},{9,5},{13... | collective-permute-start | bytes 626696 | tf_op jit(solution)/shard_map/ppermute | solution.py:28
  46.2 14.1 %collective-permute-start.4 = (f32[3,4,40,136]{3,2,1,0:T(8,128)S(1)}, f32[3,4,40,136]{3,2,1,0:T(8,128)S(1)}, u32[]{:S(2)}, u32[]{:S(2)}) collective-permute-start(f32[3,4,40,136]{3,2,1,0:T(8,128)S(1)} %get-tuple-element.27), channel_id=1, source_target_pairs={{0,1},{1,2},{2,3},{4,5},{5,6},{6,7},{8,9},{9,10},{10,11},{12,13},{... | collective-permute-start | bytes 783368 | tf_op jit(solution)/shard_map/ppermute | solution.py:26
  49.4 14.8 %collective-permute-start.5 = (f32[3,4,40,136]{3,2,1,0:T(8,128)S(1)}, f32[3,4,40,136]{3,2,1,0:T(8,128)S(1)}, u32[]{:S(2)}, u32[]{:S(2)}) collective-permute-start(f32[3,4,40,136]{3,2,1,0:T(8,128)S(1)} %get-tuple-element.28), channel_id=1, source_target_pairs={{1,0},{2,1},{3,2},{5,4},{6,5},{7,6},{9,8},{10,9},{11,10},{13,12},{... | collective-permute-start | bytes 783368 | tf_op jit(solution)/shard_map/ppermute | solution.py:28
  121.1 12.4 %collective-permute-start.8 = (f32[3,40,4,144]{3,1,2,0:T(8,128)S(1)}, f32[3,40,4,144]{3,1,2,0:T(8,128)S(1)}, u32[]{:S(2)}, u32[]{:S(2)}) collective-permute-start(f32[3,40,4,144]{3,1,2,0:T(8,128)S(1)} %get-tuple-element.23), channel_id=1, source_target_pairs={{0,4},{4,8},{8,12},{12,16},{16,20},{20,24},{24,28},{1,5},{5,9},{9,... | collective-permute-start | bytes 829448 | tf_op jit(solution)/shard_map/ppermute | solution.py:26
  125.7 20.7 %collective-permute-start.9 = (f32[3,40,4,144]{3,1,2,0:T(8,128)S(1)}, f32[3,40,4,144]{3,1,2,0:T(8,128)S(1)}, u32[]{:S(2)}, u32[]{:S(2)}) collective-permute-start(f32[3,40,4,144]{3,1,2,0:T(8,128)S(1)} %get-tuple-element.24), channel_id=1, source_target_pairs={{4,0},{8,4},{12,8},{16,12},{20,16},{24,20},{28,24},{5,1},{9,5},{13... | collective-permute-start | bytes 829448 | tf_op jit(solution)/shard_map/ppermute | solution.py:28
  147.2 14.3 %collective-permute-start.10 = (f32[3,4,48,144]{3,1,2,0:T(4,128)S(1)}, f32[3,4,48,144]{3,1,2,0:T(4,128)S(1)}, u32[]{:S(2)}, u32[]{:S(2)}) collective-permute-start(f32[3,4,48,144]{3,1,2,0:T(4,128)S(1)} %get-tuple-element.19), channel_id=1, source_target_pairs={{0,1},{1,2},{2,3},{4,5},{5,6},{6,7},{8,9},{9,10},{10,11},{12,13},{... | collective-permute-start | bytes 995336 | tf_op jit(solution)/shard_map/ppermute | solution.py:26
  150.5 15.2 %collective-permute-start.11 = (f32[3,4,48,144]{3,1,2,0:T(4,128)S(1)}, f32[3,4,48,144]{3,1,2,0:T(4,128)S(1)}, u32[]{:S(2)}, u32[]{:S(2)}) collective-permute-start(f32[3,4,48,144]{3,1,2,0:T(4,128)S(1)} %get-tuple-element.20), channel_id=1, source_target_pairs={{1,0},{2,1},{3,2},{5,4},{6,5},{7,6},{9,8},{10,9},{11,10},{13,12},{... | collective-permute-start | bytes 995336 | tf_op jit(solution)/shard_map/ppermute | solution.py:28
  173.5 12.7 %collective-permute-start.17 = (f32[3,32,32,1]{2,1,3,0:T(8,128)S(1)}, f32[3,32,32,1]{2,1,3,0:T(8,128)S(1)}, u32[]{:S(2)}, u32[]{:S(2)}) collective-permute-start(f32[3,32,32,1]{2,1,3,0:T(8,128)S(1)} %copy.105), channel_id=1, source_target_pairs={{0,32},{32,64},{64,96},{1,33},{33,65},{65,97},{2,34},{34,66},{66,9... | collective-permute-start | bytes 36872 | tf_op jit(solution)/shard_map/ppermute | solution.py:26
  177.6 11.0 %collective-permute-start.18 = (f32[3,32,32,1]{2,1,3,0:T(8,128)S(1)}, f32[3,32,32,1]{2,1,3,0:T(8,128)S(1)}, u32[]{:S(2)}, u32[]{:S(2)}) collective-permute-start(f32[3,32,32,1]{2,1,3,0:T(8,128)S(1)} %copy.106), channel_id=1, source_target_pairs={{32,0},{64,32},{96,64},{33,1},{65,33},{97,65},{34,2},{66,34},{98,6... | collective-permute-start | bytes 36872 | tf_op jit(solution)/shard_map/ppermute | solution.py:28
  181.2 16.6 %collective-permute-start.12 = (f32[32,32,1]{2,0,1:T(8,128)}, f32[32,32,1]{2,0,1:T(8,128)S(1)}, u32[]{:S(2)}, u32[]{:S(2)}) collective-permute-start(f32[32,32,1]{2,0,1:T(8,128)} %get-tuple-element.64), channel_id=1, source_target_pairs={{0,32},{32,64},{64,96},{1,33},{33,65},{65,97},{2,34},{34,66},{66,9... | collective-permute-start | bytes 12296 | tf_op jit(solution)/shard_map/ppermute | solution.py:26
  184.3 13.5 %collective-permute-start.13 = (f32[32,32,1]{2,0,1:T(8,128)}, f32[32,32,1]{2,0,1:T(8,128)S(1)}, u32[]{:S(2)}, u32[]{:S(2)}) collective-permute-start(f32[32,32,1]{2,0,1:T(8,128)} %get-tuple-element.63), channel_id=1, source_target_pairs={{32,0},{64,32},{96,64},{33,1},{65,33},{97,65},{34,2},{66,34},{98,6... | collective-permute-start | bytes 12296 | tf_op jit(solution)/shard_map/ppermute | solution.py:28
  192.2 12.8 %collective-permute-start.19 = (f32[3,32,1,130]{3,1,2,0:T(8,128)S(1)}, f32[3,32,1,130]{3,1,2,0:T(8,128)S(1)}, u32[]{:S(2)}, u32[]{:S(2)}) collective-permute-start(f32[3,32,1,130]{3,1,2,0:T(8,128)S(1)} %get-tuple-element.41), channel_id=1, source_target_pairs={{0,4},{4,8},{8,12},{12,16},{16,20},{20,24},{24,28},{1,5},{5,9},{9,... | collective-permute-start | bytes 149768 | tf_op jit(solution)/shard_map/ppermute | solution.py:26
  198.0 11.9 %collective-permute-start.14 = (f32[32,1,130]{2,0,1:T(8,128)S(1)}, f32[32,1,130]{2,0,1:T(8,128)S(1)}, u32[]{:S(2)}, u32[]{:S(2)}) collective-permute-start(f32[32,1,130]{2,0,1:T(8,128)S(1)} %get-tuple-element.58), channel_id=1, source_target_pairs={{0,4},{4,8},{8,12},{12,16},{16,20},{20,24},{24,28},{1,5},{5,9},{9,... | collective-permute-start | bytes 49928 | tf_op jit(solution)/shard_map/ppermute | solution.py:26
  231.3 9.9 %collective-permute-start.24 = (f32[3,32,32,4]{2,1,3,0:T(8,128)S(1)}, f32[3,32,32,4]{2,1,3,0:T(8,128)S(1)}, u32[]{:S(2)}, u32[]{:S(2)}) collective-permute-start(f32[3,32,32,4]{2,1,3,0:T(8,128)S(1)} %copy.110), channel_id=1, source_target_pairs={{0,32},{32,64},{64,96},{1,33},{33,65},{65,97},{2,34},{34,66},{66,9... | collective-permute-start | bytes 147464 | tf_op jit(solution)/shard_map/ppermute | solution.py:26
  251.5 12.3 %collective-permute-start.26 = (f32[3,32,4,136]{3,1,2,0:T(8,128)S(1)}, f32[3,32,4,136]{3,1,2,0:T(8,128)S(1)}, u32[]{:S(2)}, u32[]{:S(2)}) collective-permute-start(f32[3,32,4,136]{3,1,2,0:T(8,128)S(1)} %get-tuple-element.39), channel_id=1, source_target_pairs={{0,4},{4,8},{8,12},{12,16},{16,20},{20,24},{24,28},{1,5},{5,9},{9,... | collective-permute-start | bytes 626696 | tf_op jit(solution)/shard_map/ppermute | solution.py:26
  258.0 18.0 %collective-permute-start.27 = (f32[3,32,4,136]{3,1,2,0:T(8,128)S(1)}, f32[3,32,4,136]{3,1,2,0:T(8,128)S(1)}, u32[]{:S(2)}, u32[]{:S(2)}) collective-permute-start(f32[3,32,4,136]{3,1,2,0:T(8,128)S(1)} %get-tuple-element.40), channel_id=1, source_target_pairs={{4,0},{8,4},{12,8},{16,12},{20,16},{24,20},{28,24},{5,1},{9,5},{13... | collective-permute-start | bytes 626696 | tf_op jit(solution)/shard_map/ppermute | solution.py:28
  276.7 12.3 %collective-permute-start.28 = (f32[3,4,40,136]{3,1,2,0:T(4,128)S(1)}, f32[3,4,40,136]{3,1,2,0:T(4,128)S(1)}, u32[]{:S(2)}, u32[]{:S(2)}) collective-permute-start(f32[3,4,40,136]{3,1,2,0:T(4,128)S(1)} %get-tuple-element.25), channel_id=1, source_target_pairs={{0,1},{1,2},{2,3},{4,5},{5,6},{6,7},{8,9},{9,10},{10,11},{12,13},{... | collective-permute-start | bytes 783368 | tf_op jit(solution)/shard_map/ppermute | solution.py:26
  280.0 13.2 %collective-permute-start.29 = (f32[3,4,40,136]{3,1,2,0:T(4,128)S(1)}, f32[3,4,40,136]{3,1,2,0:T(4,128)S(1)}, u32[]{:S(2)}, u32[]{:S(2)}) collective-permute-start(f32[3,4,40,136]{3,1,2,0:T(4,128)S(1)} %get-tuple-element.26), channel_id=1, source_target_pairs={{1,0},{2,1},{3,2},{5,4},{6,5},{7,6},{9,8},{10,9},{11,10},{13,12},{... | collective-permute-start | bytes 783368 | tf_op jit(solution)/shard_map/ppermute | solution.py:28
  357.8 10.3 %collective-permute-start.32 = (f32[3,40,4,144]{3,1,2,0:T(8,128)S(1)}, f32[3,40,4,144]{3,1,2,0:T(8,128)S(1)}, u32[]{:S(2)}, u32[]{:S(2)}) collective-permute-start(f32[3,40,4,144]{3,1,2,0:T(8,128)S(1)} %get-tuple-element.21), channel_id=1, source_target_pairs={{0,4},{4,8},{8,12},{12,16},{16,20},{20,24},{24,28},{1,5},{5,9},{9,... | collective-permute-start | bytes 829448 | tf_op jit(solution)/shard_map/ppermute | solution.py:26
  360.7 19.9 %collective-permute-start.33 = (f32[3,40,4,144]{3,1,2,0:T(8,128)S(1)}, f32[3,40,4,144]{3,1,2,0:T(8,128)S(1)}, u32[]{:S(2)}, u32[]{:S(2)}) collective-permute-start(f32[3,40,4,144]{3,1,2,0:T(8,128)S(1)} %get-tuple-element.22), channel_id=1, source_target_pairs={{4,0},{8,4},{12,8},{16,12},{20,16},{24,20},{28,24},{5,1},{9,5},{13... | collective-permute-start | bytes 829448 | tf_op jit(solution)/shard_map/ppermute | solution.py:28
  381.4 12.6 %collective-permute-start.34 = (f32[3,4,48,144]{3,1,2,0:T(4,128)S(1)}, f32[3,4,48,144]{3,1,2,0:T(4,128)S(1)}, u32[]{:S(2)}, u32[]{:S(2)}) collective-permute-start(f32[3,4,48,144]{3,1,2,0:T(4,128)S(1)} %get-tuple-element.17), channel_id=1, source_target_pairs={{0,1},{1,2},{2,3},{4,5},{5,6},{6,7},{8,9},{9,10},{10,11},{12,13},{... | collective-permute-start | bytes 995336 | tf_op jit(solution)/shard_map/ppermute | solution.py:26
  383.3 14.8 %collective-permute-start.35 = (f32[3,4,48,144]{3,1,2,0:T(4,128)S(1)}, f32[3,4,48,144]{3,1,2,0:T(4,128)S(1)}, u32[]{:S(2)}, u32[]{:S(2)}) collective-permute-start(f32[3,4,48,144]{3,1,2,0:T(4,128)S(1)} %get-tuple-element.18), channel_id=1, source_target_pairs={{1,0},{2,1},{3,2},{5,4},{6,5},{7,6},{9,8},{10,9},{11,10},{13,12},{... | collective-permute-start | bytes 995336 | tf_op jit(solution)/shard_map/ppermute | solution.py:28
  (72 other events, 767.9 us)
where the time goes:
time: 458 us; the launch traced here: 452 us
  waiting for transfers between devices  134 us (29%)
  starting transfers between devices  109 us (24%)
  local copies, waits for them, and re-layouts  83.6 us (18%)
  matrix products  68.4 us (15%)
  other arithmetic  54.6 us (12%)
    ppermute x21, waiting for transfers between devices, with_halo(): lax.ppermute(head, axis, [((i + 1) % count, i) for i in range(ends)])  84.4 us
    ppermute x21, starting transfers between devices, with_halo(): lax.ppermute(tail, axis, [(i, (i + 1) % count) for i in range(ends)])  75.3 us
    ppermute x21, waiting for transfers between devices, with_halo(): lax.ppermute(tail, axis, [(i, (i + 1) % count) for i in range(ends)])  49.6 us
    ppermute x21, starting transfers between devices, with_halo(): lax.ppermute(head, axis, [((i + 1) % count, i) for i in range(ends)])  34 us
    slice x12, local copies, waits for them, and re-layouts, with_halo(): lax.slice_in_dim(cells, cells.shape[dim] - width, cells.shape[dim], axis=...  27.3 us
    dot_general x4, matrix products, transform_all(): return jnp.einsum('czyx,zk->ckyx', values, along_z, precision=HIGHEST)  26.9 us
    dot_general x4, matrix products, transform_all(): values = jnp.einsum('czyx,xk->czyk', values, along_x, precision=HIGHEST)  20.8 us
    dot_general x4, matrix products, transform_all(): values = jnp.einsum('czyx,yk->czkx', values, along_y, precision=HIGHEST)  19.8 us
  transfers between devices with their start and end apart: 42, of which 25 were waited for; matrix products, arithmetic and copies ran while one was open for 11% of the time, Pallas kernels for 0%

commit v1 on v0

v1 whole, which is shorter than its diff:
```python
import jax
import jax.numpy as jnp
import numpy as np
from jax import lax
from jax.experimental import pallas as pl
from jax.experimental.pallas import tpu as pltpu
from jax.sharding import PartitionSpec as P

BRICK = 32
MARGIN = 4
SWEEPS = 2
LENGTH = BRICK + 2 * MARGIN
LANES = 128
WIDE = 256
ROWS = LENGTH * LENGTH
PADDED = 1664
CHUNKS = PADDED // LANES
OWNED = BRICK * LENGTH
LAMBDA_RATIO = 2.0
SIGMA_SHIFT = 0.1
REF_MODULUS = 1.5
VOID_MODULUS = 0.1
MESH = pl.DeviceIdType.MESH
PHASES = 9
AY, AZ, AX, BX, BZ, BY, CY, CZ, CX = range(PHASES)
AXIS = {AY: "gy", AZ: "gz", AX: "gx", BX: "gx", BZ: "gz", BY: "gy", CY: "gy", CZ: "gz", CX: "gx"}
F32 = jnp.float32
BF16 = jnp.bfloat16


def ratio(component, direction):
    return LAMBDA_RATIO if component == direction else 1.0


def halves(values):
    high = values.astype(BF16)
    return high, (values - high.astype(F32)).astype(BF16)


def constants():
    grid = np.arange(1, LENGTH + 1, dtype=np.float64)
    sine = np.sqrt(2.0 / (LENGTH + 1)) * np.sin(np.pi * grid[:, None] * grid[None, :] / (LENGTH + 1))
    eigen = 2.0 - 2.0 * np.cos(np.pi * grid / (LENGTH + 1))
    spot = np.arange(LENGTH, dtype=np.float64)
    ramp = np.minimum(np.minimum((spot + 0.5) / (2 * MARGIN), (LENGTH - 0.5 - spot) / (2 * MARGIN)), 1.0)
    ramped = ramp[:, None] * sine
    place = np.concatenate([np.arange(MARGIN, MARGIN + BRICK), np.arange(MARGIN), np.arange(MARGIN + BRICK, LENGTH)])
    forward = ramped[place].T
    backward = sine.T[place]
    count = LANES // BRICK
    wide_x = LANES + 2 * MARGIN
    forward_x = np.zeros((wide_x, WIDE))
    backward_x = np.zeros((WIDE, wide_x))
    for brick in range(count):
        rows = slice(brick * BRICK, brick * BRICK + LENGTH)
        columns = slice(brick * LENGTH, (brick + 1) * LENGTH)
        forward_x[rows, columns] = ramped
        backward_x[columns, rows] = sine
    into = np.zeros((WIDE, WIDE))
    into[:LANES] = forward_x[MARGIN:MARGIN + LANES]
    into[LANES:LANES + MARGIN] = forward_x[:MARGIN]
    into[LANES + MARGIN:LANES + 2 * MARGIN] = forward_x[MARGIN + LANES:]
    out = backward_x[:, MARGIN:MARGIN + LANES]
    edge = np.concatenate([backward_x[:, :MARGIN], backward_x[:, MARGIN + LANES:]], axis=1).T
    eigen_x = np.zeros((1, WIDE))
    eigen_x[0, : count * LENGTH] = np.tile(eigen, count)
    eigen_lanes = np.broadcast_to(eigen[:, None], (LENGTH, WIDE))
    take4 = np.zeros((8, LANES))
    take1 = np.zeros((8, LANES))
    for i in range(MARGIN):
        take4[i, i] = 1.0
        take4[MARGIN + i, LANES - MARGIN + i] = 1.0
    take1[0, 0] = 1.0
    take1[1, LANES - 1] = 1.0

    def split(matrix, stack):
        matrix = matrix.astype(np.float32)
        high = matrix.astype(BF16)
        low = (matrix - high.astype(np.float32)).astype(BF16)
        return np.concatenate([high, low], axis=0) if stack else (high, low)

    return (
        split(forward, True),
        split(backward, True),
        *split(into, False),
        *split(out, False),
        split(edge, True),
        eigen_x.astype(np.float32),
        np.ascontiguousarray(eigen_lanes).astype(np.float32),
        take4.astype(BF16),
        take1.astype(BF16),
    ), eigen


def dot(a, b):
    return jnp.dot(a, b, preferred_element_type=F32)


def dot_nt(a, b):
    return lax.dot_general(a, b, (((1,), (1,)), ((), ())), preferred_element_type=F32)


def apply_left(stacked, values):
    size = LENGTH
    high, low = halves(values)
    both = dot(stacked, high)
    return both[:size] + both[size:] + dot(stacked[:size], low)


def kernel(
    load, labels, mask, table,
    fwd, bwd, into_hi, into_lo, out_hi, out_lo, edge, eigen_x, eigen_rows, take4, take1,
    disp, resid,
    modulus, faces, w, xs, xr, b1a, b1b, b2a, b2b, zb, fs, fr, zr, ys, yr, corr, rinv,
    cys, cyr, czs, czr, cxs, cxr,
    send_sem, recv_sem,
):
    index = {a: lax.axis_index(a) for a in ("gx", "gy", "gz")}
    count = {a: lax.axis_size(a) for a in ("gx", "gy", "gz")}
    lower = {a: lax.rem(index[a] + count[a] - 1, count[a]) for a in index}
    upper = {a: lax.rem(index[a] + 1, count[a]) for a in index}
    has_lower = {a: index[a] > 0 for a in index}
    has_upper = {a: index[a] < count[a] - 1 for a in index}

    barrier = pltpu.get_barrier_semaphore()
    for a in ("gx", "gy", "gz"):
        pl.semaphore_signal(barrier, inc=1, device_id={a: lower[a]}, device_id_type=MESH)
        pl.semaphore_signal(barrier, inc=1, device_id={a: upper[a]}, device_id_type=MESH)
    pl.semaphore_wait(barrier, 6)

    def copies(slot, phase, down, up):
        a = AXIS[phase]
        made = []
        for side, (source, target), device in ((0, down, lower[a]), (1, up, upper[a])):
            number = (slot * PHASES + phase) * 2 + side
            made.append(pltpu.make_async_remote_copy(
                src_ref=source, dst_ref=target,
                send_sem=send_sem.at[number], recv_sem=recv_sem.at[number],
                device_id={a: device}, device_id_type=MESH,
            ))
        return made

    pending = {}

    def send(slot, phase, down, up):
        made = copies(slot, phase, down, up)
        for copy in made:
            copy.start()
        pending[slot, phase] = made

    def arrive(slot, phase):
        for copy in pending[slot, phase]:
            copy.wait_recv()

    def keep(flag, values):
        return jnp.where(flag, values, 0.0)

    def face_columns(values):
        flat = values.reshape(BRICK * BRICK, LANES)
        high, low = halves(flat)
        return dot_nt(take1[...], high) + dot_nt(take1[...], low)

    def halo_send(slot, values):
        cys[slot, 0] = values[:, 0, :]
        cys[slot, 1] = values[:, BRICK - 1, :]
        czs[slot, 0] = values[0]
        czs[slot, 1] = values[BRICK - 1]
        cxs[slot] = face_columns(values)
        send(slot, CY, (cys.at[slot, 0], cyr.at[slot, 1]), (cys.at[slot, 1], cyr.at[slot, 0]))
        send(slot, CZ, (czs.at[slot, 0], czr.at[slot, 1]), (czs.at[slot, 1], czr.at[slot, 0]))
        send(slot, CX, (cxs.at[slot], cxr.at[slot, 1]), (cxs.at[slot], cxr.at[slot, 0]))

    def halo_get(slot):
        for phase in (CY, CZ, CX):
            arrive(slot, phase)
        low_y = keep(has_lower["gy"], cyr[slot, 0])
        high_y = keep(has_upper["gy"], cyr[slot, 1])
        low_z = keep(has_lower["gz"], czr[slot, 0])
        high_z = keep(has_upper["gz"], czr[slot, 1])
        left = keep(has_lower["gx"], cxr[slot, 0, 1:2, :])
        right = keep(has_upper["gx"], cxr[slot, 1, 0:1, :])
        side = jnp.concatenate([left, jnp.zeros((LANES - 2, BRICK * BRICK), F32), right], axis=0)
        side = jnp.concatenate(
            [jnp.transpose(side[:, i * LANES:(i + 1) * LANES]) for i in range(8)], axis=0
        ).reshape(BRICK, BRICK, LANES)
        return low_y, high_y, low_z, high_z, side

    def shifts(values, halo):
        low_y, high_y, low_z, high_z, side = halo
        lane = lax.broadcasted_iota(jnp.int32, values.shape, 2)
        yield jnp.concatenate([low_z[None], values[:-1]], axis=0)
        yield jnp.concatenate([values[1:], high_z[None]], axis=0)
        yield jnp.concatenate([low_y[:, None, :], values[:, :-1]], axis=1)
        yield jnp.concatenate([values[:, 1:], high_y[:, None, :]], axis=1)
        yield jnp.where(lane == 0, side, jnp.roll(values, 1, axis=2))
        yield jnp.where(lane == LANES - 1, side, jnp.roll(values, -1, axis=2))

    def a_start(s, c):
        slot = s * 3 + c
        values = w[slot, 0:OWNED, :].reshape(BRICK, LENGTH, LANES)
        ys[slot, 0] = values[:, 0:MARGIN, :]
        ys[slot, 1] = values[:, BRICK - MARGIN:BRICK, :]
        send(slot, AY, (ys.at[slot, 0], yr.at[slot, 1]), (ys.at[slot, 1], yr.at[slot, 0]))

    def a_z(s, c):
        slot = s * 3 + c
        arrive(slot, AY)
        low = keep(has_lower["gy"], yr[slot, 0])
        high = keep(has_upper["gy"], yr[slot, 1])
        for z in range(BRICK):
            w[slot, z * LENGTH + BRICK:(z + 1) * LENGTH, :] = jnp.concatenate([low[z], high[z]], axis=0)
        first, last = MARGIN * LENGTH, OWNED - MARGIN * LENGTH
        send(
            slot, AZ,
            (w.at[slot, pl.ds(0, first)], w.at[slot, pl.ds(OWNED + first, first)]),
            (w.at[slot, pl.ds(last, first)], w.at[slot, pl.ds(OWNED, first)]),
        )

    def a_x(s, c):
        slot = s * 3 + c
        arrive(slot, AZ)
        part = MARGIN * LENGTH
        low = w[slot, OWNED:OWNED + part, :]
        w[slot, OWNED:OWNED + part, :] = keep(has_lower["gz"], low)
        high = w[slot, OWNED + part:ROWS, :]
        w[slot, OWNED + part:ROWS, :] = keep(has_upper["gz"], high)

        def chunk(i, carry):
            at = pl.ds(pl.multiple_of(i * LANES, LANES), LANES)
            high, low = halves(w[slot, at, :])
            xs[slot, :, at] = dot_nt(take4[...], high) + dot_nt(take4[...], low)
            return carry

        lax.fori_loop(0, CHUNKS, chunk, 0)
        send(slot, AX, (xs.at[slot], xr.at[slot, 1]), (xs.at[slot], xr.at[slot, 0]))

    def solve(s, c):
        slot = s * 3 + c
        arrive(slot, AX)

        def forward_x(i, carry):
            at = pl.ds(pl.multiple_of(i * LANES, LANES), LANES)
            left = keep(has_lower["gx"], xr[slot, 0, MARGIN:, at])
            right = keep(has_upper["gx"], xr[slot, 1, :MARGIN, at])
            side = jnp.transpose(jnp.concatenate([left, right, jnp.zeros((LANES - 8, LANES), F32)], axis=0))
            high, low = halves(jnp.concatenate([w[slot, at, :], side], axis=1))
            out = dot(high, into_hi[...]) + dot(low, into_hi[...]) + dot(high, into_lo[...])
            b1a[at, :] = out[:, :LANES]
            b1b[at, :] = out[:, LANES:]
            return carry

        lax.fori_loop(0, CHUNKS, forward_x, 0)

        def forward_y(i, carry):
            for k in range(4):
                z = i * 4 + k
                at = pl.ds(pl.multiple_of(z * LENGTH, 8), LENGTH)
                out = apply_left(fwd[...], jnp.concatenate([b1a[at, :], b1b[at, :]], axis=1))
                b2a[pl.ds(z, LENGTH, stride=LENGTH), :] = out[:, :LANES]
                b2b[pl.ds(z, LENGTH, stride=LENGTH), :] = out[:, LANES:]
            return carry

        lax.fori_loop(0, LENGTH // 4, forward_y, 0)

        def solve_z(i, carry):
            for k in range(4):
                y = i * 4 + k
                at = pl.ds(pl.multiple_of(y * LENGTH, 8), LENGTH)
                out = apply_left(fwd[...], jnp.concatenate([b2a[at, :], b2b[at, :]], axis=1))
                out = apply_left(bwd[...], out * rinv[c, at, :])
                b1a[pl.ds(y, LENGTH, stride=LENGTH), :] = out[:, :LANES]
                b1b[pl.ds(y, LENGTH, stride=LENGTH), :] = out[:, LANES:]
            return carry

        lax.fori_loop(0, LENGTH // 4, solve_z, 0)

        def backward_y(i, carry):
            for k in range(4):
                z = i * 4 + k
                at = pl.ds(pl.multiple_of(z * LENGTH, 8), LENGTH)
                out = apply_left(bwd[...], jnp.concatenate([b1a[at, :], b1b[at, :]], axis=1))
                b2a[at, :] = out[:, :LANES]
                b2b[at, :] = out[:, LANES:]
            return carry

        lax.fori_loop(0, LENGTH // 4, backward_y, 0)

        def backward_x(i, carry):
            at = pl.ds(pl.multiple_of(i * LANES, LANES), LANES)
            high, low = halves(jnp.concatenate([b2a[at, :], b2b[at, :]], axis=1))
            zb[slot, at, :] = dot(high, out_hi[...]) + dot(low, out_hi[...]) + dot(high, out_lo[...])
            both = dot_nt(edge[...], high)
            fs[slot, :, at] = both[:8] + both[8:] + dot_nt(edge[0:8, :], low)
            return carry

        lax.fori_loop(0, CHUNKS, backward_x, 0)
        send(slot, BX, (fs.at[slot], fr.at[slot, 1]), (fs.at[slot], fr.at[slot, 0]))

    def b_z(s, c):
        slot = s * 3 + c
        arrive(slot, BX)

        def chunk(i, carry):
            at = pl.ds(pl.multiple_of(i * LANES, LANES), LANES)
            left = keep(has_lower["gx"], fr[slot, 0, MARGIN:, at])
            right = keep(has_upper["gx"], fr[slot, 1, :MARGIN, at])
            side = jnp.concatenate([left, jnp.zeros((LANES - 8, LANES), F32), right], axis=0)
            zb[slot, at, :] += jnp.transpose(side)
            return carry

        lax.fori_loop(0, CHUNKS, chunk, 0)
        part = MARGIN * LENGTH
        send(
            slot, BZ,
            (zb.at[slot, pl.ds(OWNED, part)], zr.at[slot, 1]),
            (zb.at[slot, pl.ds(OWNED + part, part)], zr.at[slot, 0]),
        )

    def b_y(s, c):
        slot = s * 3 + c
        arrive(slot, BZ)
        part = MARGIN * LENGTH
        zb[slot, 0:part, :] += keep(has_lower["gz"], zr[slot, 0])
        zb[slot, OWNED - part:OWNED, :] += keep(has_upper["gz"], zr[slot, 1])
        other = slot + 6
        for z in range(BRICK):
            rows = zb[slot, z * LENGTH + BRICK:(z + 1) * LENGTH, :]
            ys[other, 0, z] = rows[:MARGIN]
            ys[other, 1, z] = rows[MARGIN:]
        send(slot, BY, (ys.at[other, 0], yr.at[other, 1]), (ys.at[other, 1], yr.at[other, 0]))

    def c_start(s, c):
        slot = s * 3 + c
        arrive(slot, BY)
        other = slot + 6
        low = keep(has_lower["gy"], yr[other, 0])
        high = keep(has_upper["gy"], yr[other, 1])
        own = zb[slot, 0:OWNED, :].reshape(BRICK, LENGTH, LANES)[:, :BRICK]
        blank = jnp.zeros((BRICK, MARGIN, LANES), F32)
        own = jnp.concatenate([
            own[:, :8] + jnp.concatenate([low, blank], axis=1),
            own[:, 8:24],
            own[:, 24:] + jnp.concatenate([blank, high], axis=1),
        ], axis=1)
        corr[slot] = own
        halo_send(slot, own)
        if s == 0:
            disp[c] = own
        else:
            disp[c] += own

    def update(s, c):
        slot = s * 3 + c
        halo = halo_get(slot)
        values = corr[slot]
        total = SIGMA_SHIFT * modulus[...] * values
        for number, moved in enumerate(shifts(values, halo)):
            total = total + (ratio(c, number // 2) * 0.5) * faces[number] * (values - moved)
        if s == 0:
            old = load[c]
        else:
            old = w[slot, 0:OWNED, :].reshape(BRICK, LENGTH, LANES)[:, :BRICK]
        new = old - total
        if s == SWEEPS - 1:
            resid[c] = new
        else:
            for z in range(BRICK):
                w[slot + 3, z * LENGTH:z * LENGTH + BRICK, :] = new[z]

    for c in range(3):
        for z in range(BRICK):
            w[c, z * LENGTH:z * LENGTH + BRICK, :] = load[c, z]
    for slot in range(6):
        w[slot, ROWS:, :] = jnp.zeros((PADDED - ROWS, LANES), F32)
    for c in range(3):
        a_start(0, c)

    def look(z, carry):
        picked = labels[z]
        value = jnp.zeros(picked.shape, F32)
        for number in range(table.shape[0]):
            value = jnp.where(picked == number, table[number], value)
        modulus[z] = jnp.where(mask[z] == 1, value, VOID_MODULUS)
        return carry

    lax.fori_loop(0, BRICK, look, 0)
    halo_send(6, modulus[...])

    for c in range(3):
        def invert(y, carry, c=c):
            at = pl.ds(pl.multiple_of(y * LENGTH, 8), LENGTH)
            rinv[c, at, :] = 1.0 / (REF_MODULUS * (
                ratio(c, 0) * eigen_rows[...]
                + ratio(c, 1) * eigen_rows[pl.ds(y, 1), :]
                + ratio(c, 2) * eigen_x[...]
                + SIGMA_SHIFT
            ))
            return carry

        lax.fori_loop(0, LENGTH, invert, 0)

    own = modulus[...]
    for number, moved in enumerate(shifts(own, halo_get(6))):
        faces[number] = own + moved

    for s in range(SWEEPS):
        for stage in (a_z, a_x, solve, b_z, b_y, c_start, update):
            for c in range(3):
                stage(s, c)
                if stage is update and s < SWEEPS - 1:
                    a_start(s + 1, c)

    for made in pending.values():
        for copy in made:
            copy.wait_send()


def local(load, labels, mask, table):
    tables, _ = constants()
    vmem = pl.BlockSpec(memory_space=pltpu.VMEM)
    smem = pl.BlockSpec(memory_space=pltpu.SMEM)
    slots = 3 * SWEEPS
    field = jax.ShapeDtypeStruct(load.shape, F32)
    block = (BRICK, BRICK, LANES)
    return pl.pallas_call(
        kernel,
        out_shape=(field, field),
        in_specs=[vmem, vmem, vmem, smem] + [vmem] * len(tables),
        out_specs=(vmem, vmem),
        scratch_shapes=[
            pltpu.VMEM(block, F32),
            pltpu.VMEM((6,) + block, F32),
            pltpu.VMEM((slots, PADDED, LANES), F32),
            pltpu.VMEM((slots, 8, PADDED), F32),
            pltpu.VMEM((slots, 2, 8, PADDED), F32),
            pltpu.VMEM((PADDED, LANES), F32),
            pltpu.VMEM((PADDED, LANES), F32),
            pltpu.VMEM((PADDED, LANES), F32),
            pltpu.VMEM((PADDED, LANES), F32),
            pltpu.VMEM((slots, PADDED, LANES), F32),
            pltpu.VMEM((slots, 8, PADDED), F32),
            pltpu.VMEM((slots, 2, 8, PADDED), F32),
            pltpu.VMEM((slots, 2, MARGIN * LENGTH, LANES), F32),
            pltpu.VMEM((2 * slots, 2, BRICK, MARGIN, LANES), F32),
            pltpu.VMEM((2 * slots, 2, BRICK, MARGIN, LANES), F32),
            pltpu.VMEM((slots,) + block, F32),
            pltpu.VMEM((3, ROWS, WIDE), F32),
            pltpu.VMEM((slots + 1, 2, BRICK, LANES), F32),
            pltpu.VMEM((slots + 1, 2, BRICK, LANES), F32),
            pltpu.VMEM((slots + 1, 2, BRICK, LANES), F32),
            pltpu.VMEM((slots + 1, 2, BRICK, LANES), F32),
            pltpu.VMEM((slots + 1, 8, BRICK * BRICK), F32),
            pltpu.VMEM((slots + 1, 2, 8, BRICK * BRICK), F32),
            pltpu.SemaphoreType.DMA(((slots + 1) * PHASES * 2,)),
            pltpu.SemaphoreType.DMA(((slots + 1) * PHASES * 2,)),
        ],
        compiler_params=pltpu.CompilerParams(
            collective_id=0, has_side_effects=True, vmem_limit_bytes=62 * 1024 * 1024
        ),
    )(load, labels, mask, table, *tables)


def solution(mesh):
    placed = (P(None, "gz", "gy", "gx"), P("gz", "gy", "gx"), P("gz", "gy", "gx"), P())
    return jax.shard_map(
        local,
        mesh=mesh,
        in_specs=placed,
        out_specs=(P(None, "gz", "gy", "gx"), P(None, "gz", "gy", "gx")),
        check_vma=False,
    )
```

time: 458 us -> 213 us (0.47)
  Pallas kernels: 0 us -> 207 us
  waiting for transfers between devices: 134 us -> 0 us
  starting transfers between devices: 109 us -> 0 us
  local copies, waits for them, and re-layouts: 83.6 us -> 3.93 us
  matrix products: 68.4 us -> 0 us
  other arithmetic: 54.6 us -> 0 us
    pallas_call x0 -> x1, Pallas kernels: none -> 207 us  [local(): pl.pallas_call(kernel, out_shape=(field, field), in_specs=[vmem, vmem, vm...]
    ppermute x42 -> x0, waiting for transfers between devices: 134 us -> none  [the longest x21 84.4 us: with_halo(): lax.ppermute(head, axis, [((i + 1) % count, i) for i in range(ends)])]
    ppermute x42 -> x0, starting transfers between devices: 109 us -> none  [the longest x21 75.3 us: with_halo(): lax.ppermute(tail, axis, [(i, (i + 1) % count) for i in range(ends)])]
    dot_general x14 -> x0, matrix products: 68.4 us -> none  [the longest x4 26.9 us: transform_all(): return jnp.einsum('czyx,zk->ckyx', values, along_z, precision=HIGHEST)]
    slice x23 -> x0, local copies, waits for them, and re-layouts: 41 us -> none  [the longest x12 27.3 us: with_halo(): lax.slice_in_dim(cells, cells.shape[dim] - width, cells.shape[dim], axis=...]
    ppermute x14 -> x0, local copies, waits for them, and re-layouts: 30.8 us -> none  [the longest x7 17.6 us: with_halo(): lax.ppermute(head, axis, [((i + 1) % count, i) for i in range(ends)])]
    concatenate x7 -> x0, other arithmetic: 18.5 us -> none  [with_halo(): jnp.concatenate([lax.ppermute(tail, axis, [(i, (i + 1) % count) for i in...]
    slice x12 -> x0, other arithmetic: 14.4 us -> none  [with_halo(): lax.slice_in_dim(cells, cells.shape[dim] - width, cells.shape[dim], axis=...]
  transfers between devices with their start and end apart: 42 -> 0, of which waited for: 25 -> 0; matrix products, arithmetic and copies ran while one was open for 11% -> 0% of each run, Pallas kernels for 0% -> 0%
where the time goes in v1:
time: 213 us; the launch traced here: 212 us
  Pallas kernels  207 us (97%)
  local copies, waits for them, and re-layouts  3.93 us (2%)
    pallas_call x1, Pallas kernels, local(): pl.pallas_call(kernel, out_shape=(field, field), in_specs=[vmem, vmem, vm...  207 us

profile of v1, /device:TPU:1, one launch (start us, length us, event | category | flops | bytes accessed | tf_op | source)
XLA Modules:
  0.0 211.8 jit_solution(9043971366388994419)
XLA Ops:
  0.6 207.2 %shard_map.158 = (f32[3,32,32,128]{3,2,1,0:T(8,128)}, f32[3,32,32,128]{3,2,1,0:T(8,128)}) custom-call(f32[3,32,32,128]{3,2,1,0:T(8,128)} %load.1, s32[32,32,128]{2,1,0:T(8,128)} %labels.1, s32[32,32,128]{2,1,0:T(8,128)} %mask.1, f32[16]{0:T(128)} %table.1, bf16[80,40]{1,0:T(8,128)(2,1)} %constant.22.clone.fwd, bf16[80,40]{1,0:T(8,128)(2,1)} %constant.23.clone.bwd, ...), custom_call_target="tpu_custom_call" | custom-call | tf_op jit(solution)/shard_map/pallas_call | solution.py:425
  207.9 0.0 copy-start
  207.9 2.8 %copy.19 = f32[3,32,32,128]{3,2,1,0:T(8,128)} copy(f32[3,32,32,128]{3,2,1,0:T(8,128)} %get-tuple-element.4) | data formatting | bytes 3145728
  210.7 0.0 copy-done
  210.7 1.1 copy.20
Async XLA Ops:
  207.9 2.8 %copy-start = (f32[3,32,32,128]{3,2,1,0:T(8,128)S(1)}, f32[3,32,32,128]{3,2,1,0:T(8,128)}, u32[]{:S(2)}) copy-start(f32[3,32,32,128]{3,2,1,0:T(8,128)} %get-tuple-element.5) | copy-start | bytes 4718596

commit v2 on v1

--- a/solution.py
+++ b/solution.py
@@ -21,6 +21,7 @@
 REF_MODULUS = 1.5
 VOID_MODULUS = 0.1
 MESH = pl.DeviceIdType.MESH
+UNROLL = 5
 PHASES = 9
 AY, AZ, AX, BX, BZ, BY, CY, CZ, CX = range(PHASES)
 AXIS = {AY: "gy", AZ: "gz", AX: "gx", BX: "gx", BZ: "gz", BY: "gy", CY: "gy", CZ: "gz", CX: "gx"}
@@ -56,60 +57,55 @@
         columns = slice(brick * LENGTH, (brick + 1) * LENGTH)
         forward_x[rows, columns] = ramped
         backward_x[columns, rows] = sine
-    into = np.zeros((WIDE, WIDE))
-    into[:LANES] = forward_x[MARGIN:MARGIN + LANES]
-    into[LANES:LANES + MARGIN] = forward_x[:MARGIN]
-    into[LANES + MARGIN:LANES + 2 * MARGIN] = forward_x[MARGIN + LANES:]
-    out = backward_x[:, MARGIN:MARGIN + LANES]
-    edge = np.concatenate([backward_x[:, :MARGIN], backward_x[:, MARGIN + LANES:]], axis=1).T
+    edge = slice(LANES, LANES + 2 * MARGIN)
+    into = forward_x[MARGIN:MARGIN + LANES]
+    into_edge = np.concatenate([forward_x[:MARGIN], forward_x[MARGIN + LANES:]])
+    out = np.zeros((WIDE, WIDE))
+    out[:, :LANES] = backward_x[:, MARGIN:MARGIN + LANES]
+    out[:, edge] = np.concatenate([backward_x[:, :MARGIN], backward_x[:, MARGIN + LANES:]], axis=1)
+    rest = count * LENGTH - LANES
     eigen_x = np.zeros((1, WIDE))
     eigen_x[0, : count * LENGTH] = np.tile(eigen, count)
     eigen_lanes = np.broadcast_to(eigen[:, None], (LENGTH, WIDE))
-    take4 = np.zeros((8, LANES))
-    take1 = np.zeros((8, LANES))
-    for i in range(MARGIN):
-        take4[i, i] = 1.0
-        take4[MARGIN + i, LANES - MARGIN + i] = 1.0
-    take1[0, 0] = 1.0
-    take1[1, LANES - 1] = 1.0
-
-    def split(matrix, stack):
-        matrix = matrix.astype(np.float32)
-        high = matrix.astype(BF16)
-        low = (matrix - high.astype(np.float32)).astype(BF16)
-        return np.concatenate([high, low], axis=0) if stack else (high, low)
-
-    return (
-        split(forward, True),
-        split(backward, True),
-        *split(into, False),
-        *split(out, False),
-        split(edge, True),
-        eigen_x.astype(np.float32),
-        np.ascontiguousarray(eigen_lanes).astype(np.float32),
-        take4.astype(BF16),
-        take1.astype(BF16),
-    ), eigen
+
+    def high(matrix):
+        return matrix.astype(np.float32).astype(BF16).astype(np.float64)
+
+    def low(matrix):
+        return matrix - high(matrix)
+
+    def pair(matrix):
+        zero = np.zeros((LENGTH, LENGTH))
+        both = np.block([[matrix, zero], [zero, matrix]])
+        return np.concatenate([high(both), high(both), low(both)], axis=1)
+
+    def tall(*parts):
+        blank = np.zeros((2 * LANES - sum(p.shape[0] for p in parts), WIDE))
+        return np.concatenate(parts + (blank,))
+
+    head, tail = out[:LANES], out[LANES:LANES + rest]
+    return [m.astype(BF16) for m in (
+        pair(forward),
+        pair(backward),
+        tall(high(into), high(into)),
+        tall(low(into), high(into_edge), high(into_edge), low(into_edge)),
+        tall(high(head), high(head)),
+        tall(low(head), high(tail), high(tail), low(tail)),
+    )] + [eigen_x.astype(np.float32), np.ascontiguousarray(eigen_lanes).astype(np.float32)]
 
 
 def dot(a, b):
     return jnp.dot(a, b, preferred_element_type=F32)
 
 
-def dot_nt(a, b):
-    return lax.dot_general(a, b, (((1,), (1,)), ((), ())), preferred_element_type=F32)
-
-
-def apply_left(stacked, values):
-    size = LENGTH
+def triple(values):
     high, low = halves(values)
-    both = dot(stacked, high)
-    return both[:size] + both[size:] + dot(stacked[:size], low)
+    return jnp.concatenate([high, low, high], axis=0)
 
 
 def kernel(
     load, labels, mask, table,
-    fwd, bwd, into_hi, into_lo, out_hi, out_lo, edge, eigen_x, eigen_rows, take4, take1,
+    fwd, bwd, into_1, into_2, out_1, out_2, eigen_x, eigen_rows,
     disp, resid,
     modulus, faces, w, xs, xr, b1a, b1b, b2a, b2b, zb, fs, fr, zr, ys, yr, corr, rinv,
     cys, cyr, czs, czr, cxs, cxr,
@@ -155,10 +151,15 @@
     def keep(flag, values):
         return jnp.where(flag, values, 0.0)
 
+    lanes = lax.broadcasted_iota(jnp.int32, (LANES, LANES), 1)
+
     def face_columns(values):
         flat = values.reshape(BRICK * BRICK, LANES)
-        high, low = halves(flat)
-        return dot_nt(take1[...], high) + dot_nt(take1[...], low)
+        total = jnp.zeros((LANES, LANES), F32)
+        for i in range(8):
+            part = pltpu.roll(flat[i * LANES:(i + 1) * LANES], 2 * i + 1, 1)
+            total = jnp.where((lanes == 2 * i) | (lanes == 2 * i + 1), part, total)
+        return jnp.transpose(total)[:16]
 
     def halo_send(slot, values):
         cys[slot, 0] = values[:, 0, :]
@@ -177,11 +178,13 @@
         high_y = keep(has_upper["gy"], cyr[slot, 1])
         low_z = keep(has_lower["gz"], czr[slot, 0])
         high_z = keep(has_upper["gz"], czr[slot, 1])
-        left = keep(has_lower["gx"], cxr[slot, 0, 1:2, :])
-        right = keep(has_upper["gx"], cxr[slot, 1, 0:1, :])
-        side = jnp.concatenate([left, jnp.zeros((LANES - 2, BRICK * BRICK), F32), right], axis=0)
+        left = keep(has_lower["gx"], cxr[slot, 0])
+        right = keep(has_upper["gx"], cxr[slot, 1])
+        odd = lax.rem(lax.broadcasted_iota(jnp.int32, (16, LANES), 0), 2) == 1
+        both = jnp.where(odd, pltpu.roll(left, 1, 0), pltpu.roll(right, 15, 0))
+        side = jnp.transpose(jnp.concatenate([both, jnp.zeros((LANES - 16, LANES), F32)], axis=0))
         side = jnp.concatenate(
-            [jnp.transpose(side[:, i * LANES:(i + 1) * LANES]) for i in range(8)], axis=0
+            [pltpu.roll(side, LANES - 1 - 2 * i, 1) for i in range(8)], axis=0
         ).reshape(BRICK, BRICK, LANES)
         return low_y, high_y, low_z, high_z, side
 
@@ -192,8 +195,8 @@
         yield jnp.concatenate([values[1:], high_z[None]], axis=0)
         yield jnp.concatenate([low_y[:, None, :], values[:, :-1]], axis=1)
         yield jnp.concatenate([values[:, 1:], high_y[:, None, :]], axis=1)
-        yield jnp.where(lane == 0, side, jnp.roll(values, 1, axis=2))
-        yield jnp.where(lane == LANES - 1, side, jnp.roll(values, -1, axis=2))
+        yield jnp.where(lane == 0, side, pltpu.roll(values, 1, 2))
+        yield jnp.where(lane == LANES - 1, side, pltpu.roll(values, LANES - 1, 2))
 
     def a_start(s, c):
         slot = s * 3 + c
@@ -225,90 +228,97 @@
         high = w[slot, OWNED + part:ROWS, :]
         w[slot, OWNED + part:ROWS, :] = keep(has_upper["gz"], high)
 
-        def chunk(i, carry):
-            at = pl.ds(pl.multiple_of(i * LANES, LANES), LANES)
+        total = jnp.zeros((LANES, LANES), F32)
+        for i in range(CHUNKS):
+            part = pltpu.roll(w[slot, i * LANES:(i + 1) * LANES, :], 8 * i + MARGIN, 1)
+            total = jnp.where((lanes >= 8 * i) & (lanes < 8 * i + 8), part, total)
+        total = jnp.transpose(total)[:CHUNKS * 8].reshape(CHUNKS, 8, LANES)
+        xs[slot, 0] = total[:, MARGIN:]
+        xs[slot, 1] = total[:, :MARGIN]
+        send(slot, AX, (xs.at[slot, 0], xr.at[slot, 1]), (xs.at[slot, 1], xr.at[slot, 0]))
+
+    def solve(s, c):
+        slot = s * 3 + c
+        arrive(slot, AX)
+
+        near = jnp.concatenate([keep(has_lower["gx"], xr[slot, 0]), keep(has_upper["gx"], xr[slot, 1])], axis=1)
+        high = near.astype(BF16).astype(F32)
+        near = jnp.concatenate([high, near - high, high], axis=1)
+        sides = []
+        for first in range(0, CHUNKS, 5):
+            rows = near[first:first + 5].reshape(-1, LANES)
+            blank = jnp.zeros((LANES - rows.shape[0], LANES), F32)
+            sides.append(jnp.transpose(jnp.concatenate([rows, blank], axis=0)))
+        for i in range(CHUNKS):
+            at = pl.ds(i * LANES, LANES)
+            side = sides[i // 5]
+            if i % 5:
+                side = pltpu.roll(side, LANES - 24 * (i % 5), 1)
             high, low = halves(w[slot, at, :])
-            xs[slot, :, at] = dot_nt(take4[...], high) + dot_nt(take4[...], low)
-            return carry
-
-        lax.fori_loop(0, CHUNKS, chunk, 0)
-        send(slot, AX, (xs.at[slot], xr.at[slot, 1]), (xs.at[slot], xr.at[slot, 0]))
-
-    def solve(s, c):
-        slot = s * 3 + c
-        arrive(slot, AX)
-
-        def forward_x(i, carry):
-            at = pl.ds(pl.multiple_of(i * LANES, LANES), LANES)
-            left = keep(has_lower["gx"], xr[slot, 0, MARGIN:, at])
-            right = keep(has_upper["gx"], xr[slot, 1, :MARGIN, at])
-            side = jnp.transpose(jnp.concatenate([left, right, jnp.zeros((LANES - 8, LANES), F32)], axis=0))
-            high, low = halves(jnp.concatenate([w[slot, at, :], side], axis=1))
-            out = dot(high, into_hi[...]) + dot(low, into_hi[...]) + dot(high, into_lo[...])
+            out = dot(jnp.concatenate([high, low], axis=1), into_1[...])
+            out += dot(jnp.concatenate([high, side.astype(BF16)], axis=1), into_2[...])
             b1a[at, :] = out[:, :LANES]
             b1b[at, :] = out[:, LANES:]
-            return carry
-
-        lax.fori_loop(0, CHUNKS, forward_x, 0)
-
-        def forward_y(i, carry):
-            for k in range(4):
-                z = i * 4 + k
-                at = pl.ds(pl.multiple_of(z * LENGTH, 8), LENGTH)
-                out = apply_left(fwd[...], jnp.concatenate([b1a[at, :], b1b[at, :]], axis=1))
-                b2a[pl.ds(z, LENGTH, stride=LENGTH), :] = out[:, :LANES]
-                b2b[pl.ds(z, LENGTH, stride=LENGTH), :] = out[:, LANES:]
-            return carry
-
-        lax.fori_loop(0, LENGTH // 4, forward_y, 0)
-
-        def solve_z(i, carry):
-            for k in range(4):
-                y = i * 4 + k
-                at = pl.ds(pl.multiple_of(y * LENGTH, 8), LENGTH)
-                out = apply_left(fwd[...], jnp.concatenate([b2a[at, :], b2b[at, :]], axis=1))
-                out = apply_left(bwd[...], out * rinv[c, at, :])
-                b1a[pl.ds(y, LENGTH, stride=LENGTH), :] = out[:, :LANES]
-                b1b[pl.ds(y, LENGTH, stride=LENGTH), :] = out[:, LANES:]
-            return carry
-
-        lax.fori_loop(0, LENGTH // 4, solve_z, 0)
-
-        def backward_y(i, carry):
-            for k in range(4):
-                z = i * 4 + k
-                at = pl.ds(pl.multiple_of(z * LENGTH, 8), LENGTH)
-                out = apply_left(bwd[...], jnp.concatenate([b1a[at, :], b1b[at, :]], axis=1))
-                b2a[at, :] = out[:, :LANES]
-                b2b[at, :] = out[:, LANES:]
-            return carry
-
-        lax.fori_loop(0, LENGTH // 4, backward_y, 0)
-
-        def backward_x(i, carry):
-            at = pl.ds(pl.multiple_of(i * LANES, LANES), LANES)
-            high, low = halves(jnp.concatenate([b2a[at, :], b2b[at, :]], axis=1))
-            zb[slot, at, :] = dot(high, out_hi[...]) + dot(low, out_hi[...]) + dot(high, out_lo[...])
-            both = dot_nt(edge[...], high)
-            fs[slot, :, at] = both[:8] + both[8:] + dot_nt(edge[0:8, :], low)
-            return carry
-
-        lax.fori_loop(0, CHUNKS, backward_x, 0)
-        send(slot, BX, (fs.at[slot], fr.at[slot, 1]), (fs.at[slot], fr.at[slot, 0]))
+
+        def transform(matrix, source, target, strided, scale=None):
+            def body(i, carry):
+                outs = []
+                for k in range(UNROLL):
+                    at = pl.ds(pl.multiple_of((i * UNROLL + k) * 2 * LENGTH, 8), 2 * LENGTH)
+                    values = jnp.concatenate([source[0][at, :], source[1][at, :]], axis=1)
+                    outs.append(dot(matrix[...], triple(values)))
+                for k in range(UNROLL):
+                    at = pl.ds(pl.multiple_of((i * UNROLL + k) * 2 * LENGTH, 8), 2 * LENGTH)
+                    out = outs[k]
+                    if scale is not None:
+                        out = out * scale[c, at, :]
+                    for half in range(2):
+                        part = out[:, half * LANES:(half + 1) * LANES]
+                        if strided:
+                            for which in range(2):
+                                spot = pl.ds((i * UNROLL + k) * 2 + which, LENGTH, stride=LENGTH)
+                                target[half][spot, :] = part[which * LENGTH:(which + 1) * LENGTH]
+                        else:
+                            target[half][at, :] = part
+                return carry
+
+            lax.fori_loop(0, LENGTH // 2 // UNROLL, body, 0)
+
+        one, two = (b1a, b1b), (b2a, b2b)
+        transform(fwd, one, two, True)
+        transform(fwd, two, one, False, rinv)
+        transform(bwd, one, two, True)
+        transform(bwd, two, one, False)
+
+        margin = jnp.zeros((LANES, LANES), F32)
+        for i in range(CHUNKS):
+            at = pl.ds(i * LANES, LANES)
+            high, low = halves(b1a[at, :])
+            tail = b1b[at, :]
+            tail_high = tail.astype(BF16).astype(F32)
+            packed = tail_high + pltpu.roll(tail - tail_high, 32, 1) + pltpu.roll(tail_high, 64, 1)
+            out = dot(jnp.concatenate([high, low], axis=1), out_1[...])
+            out += dot(jnp.concatenate([high, packed.astype(BF16)], axis=1), out_2[...])
+            zb[slot, at, :] = out[:, :LANES]
+            part = out[:, LANES:]
+            margin += pltpu.roll(part, 8 * i, 1) if i else part
+        margin = jnp.transpose(margin)[:CHUNKS * 8].reshape(CHUNKS, 8, LANES)
+        fs[slot, 0] = margin[:, :MARGIN]
+        fs[slot, 1] = margin[:, MARGIN:]
+        send(slot, BX, (fs.at[slot, 0], fr.at[slot, 1]), (fs.at[slot, 1], fr.at[slot, 0]))
 
     def b_z(s, c):
         slot = s * 3 + c
         arrive(slot, BX)
 
-        def chunk(i, carry):
-            at = pl.ds(pl.multiple_of(i * LANES, LANES), LANES)
-            left = keep(has_lower["gx"], fr[slot, 0, MARGIN:, at])
-            right = keep(has_upper["gx"], fr[slot, 1, :MARGIN, at])
-            side = jnp.concatenate([left, jnp.zeros((LANES - 8, LANES), F32), right], axis=0)
-            zb[slot, at, :] += jnp.transpose(side)
-            return carry
-
-        lax.fori_loop(0, CHUNKS, chunk, 0)
+        near = jnp.concatenate([keep(has_upper["gx"], fr[slot, 1]), keep(has_lower["gx"], fr[slot, 0])], axis=1)
+        blank = jnp.zeros((LANES - CHUNKS * 8, LANES), F32)
+        side = jnp.transpose(jnp.concatenate([near.reshape(CHUNKS * 8, LANES), blank], axis=0))
+        edge = (lanes < MARGIN) | (lanes >= LANES - MARGIN)
+        for i in range(CHUNKS):
+            at = pl.ds(i * LANES, LANES)
+            zb[slot, at, :] += jnp.where(edge, pltpu.roll(side, LANES - 8 * i - MARGIN, 1), 0.0)
+
         part = MARGIN * LENGTH
         send(
             slot, BZ,
@@ -416,7 +426,7 @@
 
 
 def local(load, labels, mask, table):
-    tables, _ = constants()
+    tables = constants()
     vmem = pl.BlockSpec(memory_space=pltpu.VMEM)
     smem = pl.BlockSpec(memory_space=pltpu.SMEM)
     slots = 3 * SWEEPS
@@ -431,15 +441,15 @@
             pltpu.VMEM(block, F32),
             pltpu.VMEM((6,) + block, F32),
             pltpu.VMEM((slots, PADDED, LANES), F32),
-            pltpu.VMEM((slots, 8, PADDED), F32),
-            pltpu.VMEM((slots, 2, 8, PADDED), F32),
+            pltpu.VMEM((slots, 2, CHUNKS, MARGIN, LANES), F32),
+            pltpu.VMEM((slots, 2, CHUNKS, MARGIN, LANES), F32),
             pltpu.VMEM((PADDED, LANES), F32),
             pltpu.VMEM((PADDED, LANES), F32),
             pltpu.VMEM((PADDED, LANES), F32),
             pltpu.VMEM((PADDED, LANES), F32),
             pltpu.VMEM((slots, PADDED, LANES), F32),
-            pltpu.VMEM((slots, 8, PADDED), F32),
-            pltpu.VMEM((slots, 2, 8, PADDED), F32),
+            pltpu.VMEM((slots, 2, CHUNKS, MARGIN, LANES), F32),
+            pltpu.VMEM((slots, 2, CHUNKS, MARGIN, LANES), F32),
             pltpu.VMEM((slots, 2, MARGIN * LENGTH, LANES), F32),
             pltpu.VMEM((2 * slots, 2, BRICK, MARGIN, LANES), F32),
             pltpu.VMEM((2 * slots, 2, BRICK, MARGIN, LANES), F32),
@@ -449,8 +459,8 @@
             pltpu.VMEM((slots + 1, 2, BRICK, LANES), F32),
             pltpu.VMEM((slots + 1, 2, BRICK, LANES), F32),
             pltpu.VMEM((slots + 1, 2, BRICK, LANES), F32),
-            pltpu.VMEM((slots + 1, 8, BRICK * BRICK), F32),
-            pltpu.VMEM((slots + 1, 2, 8, BRICK * BRICK), F32),
+            pltpu.VMEM((slots + 1, 16, LANES), F32),
+            pltpu.VMEM((slots + 1, 2, 16, LANES), F32),
             pltpu.SemaphoreType.DMA(((slots + 1) * PHASES * 2,)),
             pltpu.SemaphoreType.DMA(((slots + 1) * PHASES * 2,)),
         ],

time: 213 us -> 128 us (0.60)
  Pallas kernels: 207 us -> 123 us
    pallas_call x1, Pallas kernels: 207 us -> 123 us  [local(): pl.pallas_call(kernel, out_shape=(field, field), in_specs=[vmem, vmem, vm...]
where the time goes in v2:
time: 128 us; the launch traced here: 127 us
  Pallas kernels  123 us (96%)
  local copies, waits for them, and re-layouts  3.93 us (3%)
    pallas_call x1, Pallas kernels, local(): pl.pallas_call(kernel, out_shape=(field, field), in_specs=[vmem, vmem, vm...  123 us
    unnamed x4, local copies, waits for them, and re-layouts  3.93 us

profile of v2, /device:TPU:1, one launch (start us, length us, event | category | flops | bytes accessed | tf_op | source)
XLA Modules:
  0.0 127.3 jit_solution(2235833508676162756)
XLA Ops:
  0.6 122.7 %shard_map.131 = (f32[3,32,32,128]{3,2,1,0:T(8,128)}, f32[3,32,32,128]{3,2,1,0:T(8,128)}) custom-call(f32[3,32,32,128]{3,2,1,0:T(8,128)} %load.1, s32[32,32,128]{2,1,0:T(8,128)} %labels.1, s32[32,32,128]{2,1,0:T(8,128)} %mask.1, f32[16]{0:T(128)} %table.1, bf16[80,240]{1,0:T(8,128)(2,1)} %constant.16.clone.fwd, bf16[80,240]{1,0:T(8,128)(2,1)} %constant.17.clone.bwd, ...), custom_call_target="tpu_custom_call" | custom-call | tf_op jit(solution)/shard_map/pallas_call | solution.py:435
  123.4 0.0 copy-start
  123.4 2.8 %copy.16 = f32[3,32,32,128]{3,2,1,0:T(8,128)} copy(f32[3,32,32,128]{3,2,1,0:T(8,128)} %get-tuple-element.4) | data formatting | bytes 3145728
  126.2 0.0 copy-done
  126.2 1.1 copy.17
Async XLA Ops:
  123.4 2.8 %copy-start = (f32[3,32,32,128]{3,2,1,0:T(8,128)S(1)}, f32[3,32,32,128]{3,2,1,0:T(8,128)}, u32[]{:S(2)}) copy-start(f32[3,32,32,128]{3,2,1,0:T(8,128)} %get-tuple-element.5) | copy-start | bytes 4718596

commit v3 on v2

--- a/solution.py
+++ b/solution.py
@@ -25,6 +25,16 @@
 PHASES = 9
 AY, AZ, AX, BX, BZ, BY, CY, CZ, CX = range(PHASES)
 AXIS = {AY: "gy", AZ: "gz", AX: "gx", BX: "gx", BZ: "gz", BY: "gy", CY: "gy", CZ: "gz", CX: "gx"}
+ORDER = (
+    (0, 0, "a_z"), (0, 1, "a_z"), (0, 0, "a_x"), (0, 2, "a_z"), (0, 0, "s1"), (0, 1, "a_x"), (0, 0, "s2"),
+    (0, 2, "a_x"), (0, 0, "s3"), (0, 1, "s1"), (0, 0, "b_z"), (0, 1, "s2"), (0, 1, "s3"), (0, 0, "b_y"),
+    (0, 2, "s1"), (0, 1, "b_z"), (0, 2, "s2"), (0, 2, "s3"), (0, 0, "c_start"), (0, 1, "b_y"), (0, 2, "b_z"),
+    (0, 0, "update"), (0, 1, "c_start"), (0, 2, "b_y"), (0, 1, "update"), (1, 0, "a_z"), (0, 2, "c_start"),
+    (1, 0, "a_x"), (1, 1, "a_z"), (0, 2, "update"), (1, 0, "s1"), (1, 1, "a_x"), (1, 0, "s2"), (1, 0, "s3"),
+    (1, 2, "a_z"), (1, 1, "s1"), (1, 0, "b_z"), (1, 1, "s2"), (1, 2, "a_x"), (1, 1, "s3"), (1, 0, "b_y"),
+    (1, 2, "s1"), (1, 1, "b_z"), (1, 2, "s2"), (1, 2, "s3"), (1, 0, "c_start"), (1, 1, "b_y"), (1, 2, "b_z"),
+    (1, 0, "update"), (1, 2, "b_y"), (1, 1, "c_start"), (1, 2, "c_start"), (1, 1, "update"), (1, 2, "update"),
+)
 F32 = jnp.float32
 BF16 = jnp.bfloat16
 
@@ -200,7 +210,10 @@
 
     def a_start(s, c):
         slot = s * 3 + c
-        values = w[slot, 0:OWNED, :].reshape(BRICK, LENGTH, LANES)
+        if s == 0:
+            values = load[c]
+        else:
+            values = w[slot, 0:OWNED, :].reshape(BRICK, LENGTH, LANES)
         ys[slot, 0] = values[:, 0:MARGIN, :]
         ys[slot, 1] = values[:, BRICK - MARGIN:BRICK, :]
         send(slot, AY, (ys.at[slot, 0], yr.at[slot, 1]), (ys.at[slot, 1], yr.at[slot, 0]))
@@ -237,7 +250,33 @@
         xs[slot, 1] = total[:, :MARGIN]
         send(slot, AX, (xs.at[slot, 0], xr.at[slot, 1]), (xs.at[slot, 1], xr.at[slot, 0]))
 
-    def solve(s, c):
+    one, two = (b1a, b1b), (b2a, b2b)
+
+    def transform(matrix, source, target, strided, scale=None):
+        def body(i, carry):
+            outs = []
+            for k in range(UNROLL):
+                at = pl.ds(pl.multiple_of((i * UNROLL + k) * 2 * LENGTH, 8), 2 * LENGTH)
+                values = jnp.concatenate([source[0][at, :], source[1][at, :]], axis=1)
+                outs.append(dot(matrix[...], triple(values)))
+            for k in range(UNROLL):
+                at = pl.ds(pl.multiple_of((i * UNROLL + k) * 2 * LENGTH, 8), 2 * LENGTH)
+                out = outs[k]
+                if scale is not None:
+                    out = out * scale[at, :]
+                for half in range(2):
+                    part = out[:, half * LANES:(half + 1) * LANES]
+                    if strided:
+                        for which in range(2):
+                            spot = pl.ds((i * UNROLL + k) * 2 + which, LENGTH, stride=LENGTH)
+                            target[half][spot, :] = part[which * LENGTH:(which + 1) * LENGTH]
+                    else:
+                        target[half][at, :] = part
+            return carry
+
+        lax.fori_loop(0, LENGTH // 2 // UNROLL, body, 0)
+
+    def s1(s, c):
         slot = s * 3 + c
         arrive(slot, AX)
 
@@ -260,34 +299,14 @@
             b1a[at, :] = out[:, :LANES]
             b1b[at, :] = out[:, LANES:]
 
-        def transform(matrix, source, target, strided, scale=None):
-            def body(i, carry):
-                outs = []
-                for k in range(UNROLL):
-                    at = pl.ds(pl.multiple_of((i * UNROLL + k) * 2 * LENGTH, 8), 2 * LENGTH)
-                    values = jnp.concatenate([source[0][at, :], source[1][at, :]], axis=1)
-                    outs.append(dot(matrix[...], triple(values)))
-                for k in range(UNROLL):
-                    at = pl.ds(pl.multiple_of((i * UNROLL + k) * 2 * LENGTH, 8), 2 * LENGTH)
-                    out = outs[k]
-                    if scale is not None:
-                        out = out * scale[c, at, :]
-                    for half in range(2):
-                        part = out[:, half * LANES:(half + 1) * LANES]
-                        if strided:
-                            for which in range(2):
-                                spot = pl.ds((i * UNROLL + k) * 2 + which, LENGTH, stride=LENGTH)
-                                target[half][spot, :] = part[which * LENGTH:(which + 1) * LENGTH]
-                        else:
-                            target[half][at, :] = part
-                return carry
-
-            lax.fori_loop(0, LENGTH // 2 // UNROLL, body, 0)
-
-        one, two = (b1a, b1b), (b2a, b2b)
         transform(fwd, one, two, True)
-        transform(fwd, two, one, False, rinv)
+
+    def s2(s, c):
+        transform(fwd, two, one, False, rinv.at[c])
         transform(bwd, one, two, True)
+
+    def s3(s, c):
+        slot = s * 3 + c
         transform(bwd, two, one, False)
 
         margin = jnp.zeros((LANES, LANES), F32)
@@ -378,12 +397,12 @@
                 w[slot + 3, z * LENGTH:z * LENGTH + BRICK, :] = new[z]
 
     for c in range(3):
+        a_start(0, c)
+    for c in range(3):
         for z in range(BRICK):
             w[c, z * LENGTH:z * LENGTH + BRICK, :] = load[c, z]
     for slot in range(6):
         w[slot, ROWS:, :] = jnp.zeros((PADDED - ROWS, LANES), F32)
-    for c in range(3):
-        a_start(0, c)
 
     def look(z, carry):
         picked = labels[z]
@@ -413,12 +432,11 @@
     for number, moved in enumerate(shifts(own, halo_get(6))):
         faces[number] = own + moved
 
-    for s in range(SWEEPS):
-        for stage in (a_z, a_x, solve, b_z, b_y, c_start, update):
-            for c in range(3):
-                stage(s, c)
-                if stage is update and s < SWEEPS - 1:
-                    a_start(s + 1, c)
+    stages = dict(a_z=a_z, a_x=a_x, s1=s1, s2=s2, s3=s3, b_z=b_z, b_y=b_y, c_start=c_start, update=update)
+    for s, c, name in ORDER:
+        stages[name](s, c)
+        if name == "update" and s < SWEEPS - 1:
+            a_start(s + 1, c)
 
     for made in pending.values():
         for copy in made:

time: 128 us -> 119 us (0.930)
  Pallas kernels: 123 us -> 114 us
    pallas_call x1, Pallas kernels: 123 us -> 114 us  [local(): pl.pallas_call(kernel, out_shape=(field, field), in_specs=[vmem, vmem, vm...]
where the time goes in v3:
time: 119 us
  Pallas kernels  114 us (96%)
  local copies, waits for them, and re-layouts  3.93 us (3%)
    pallas_call x1, Pallas kernels, local(): pl.pallas_call(kernel, out_shape=(field, field), in_specs=[vmem, vmem, vm...  114 us
    unnamed x4, local copies, waits for them, and re-layouts  3.93 us

profile of v3, /device:TPU:1, one launch (start us, length us, event | category | flops | bytes accessed | tf_op | source)
XLA Modules:
  0.0 119.1 jit_solution(310575388295090874)
XLA Ops:
  0.6 114.5 %shard_map.131 = (f32[3,32,32,128]{3,2,1,0:T(8,128)}, f32[3,32,32,128]{3,2,1,0:T(8,128)}) custom-call(f32[3,32,32,128]{3,2,1,0:T(8,128)} %load.1, s32[32,32,128]{2,1,0:T(8,128)} %labels.1, s32[32,32,128]{2,1,0:T(8,128)} %mask.1, f32[16]{0:T(128)} %table.1, bf16[80,240]{1,0:T(8,128)(2,1)} %constant.16.clone.fwd, bf16[80,240]{1,0:T(8,128)(2,1)} %constant.17.clone.bwd, ...), custom_call_target="tpu_custom_call" | custom-call | tf_op jit(solution)/shard_map/pallas_call | solution.py:453
  115.1 0.0 copy-start
  115.1 2.8 %copy.16 = f32[3,32,32,128]{3,2,1,0:T(8,128)} copy(f32[3,32,32,128]{3,2,1,0:T(8,128)} %get-tuple-element.4) | data formatting | bytes 3145728
  117.9 0.0 copy-done
  117.9 1.1 copy.17
Async XLA Ops:
  115.1 2.8 %copy-start = (f32[3,32,32,128]{3,2,1,0:T(8,128)S(1)}, f32[3,32,32,128]{3,2,1,0:T(8,128)}, u32[]{:S(2)}) copy-start(f32[3,32,32,128]{3,2,1,0:T(8,128)} %get-tuple-element.5) | copy-start | bytes 4718596

commit v4 on v3

--- a/solution.py
+++ b/solution.py
@@ -22,18 +22,20 @@
 VOID_MODULUS = 0.1
 MESH = pl.DeviceIdType.MESH
 UNROLL = 5
-PHASES = 9
-AY, AZ, AX, BX, BZ, BY, CY, CZ, CX = range(PHASES)
-AXIS = {AY: "gy", AZ: "gz", AX: "gx", BX: "gx", BZ: "gz", BY: "gy", CY: "gy", CZ: "gz", CX: "gx"}
+PHASES = 10
+AY, AZ, AE, AX, BX, BZ, BY, CY, CZ, CX = range(PHASES)
+AXIS = ("gy", "gz", "gz", "gx", "gx", "gz", "gy", "gy", "gz", "gx")
+PLANES = 42
 ORDER = (
-    (0, 0, "a_z"), (0, 1, "a_z"), (0, 0, "a_x"), (0, 2, "a_z"), (0, 0, "s1"), (0, 1, "a_x"), (0, 0, "s2"),
-    (0, 2, "a_x"), (0, 0, "s3"), (0, 1, "s1"), (0, 0, "b_z"), (0, 1, "s2"), (0, 1, "s3"), (0, 0, "b_y"),
-    (0, 2, "s1"), (0, 1, "b_z"), (0, 2, "s2"), (0, 2, "s3"), (0, 0, "c_start"), (0, 1, "b_y"), (0, 2, "b_z"),
-    (0, 0, "update"), (0, 1, "c_start"), (0, 2, "b_y"), (0, 1, "update"), (1, 0, "a_z"), (0, 2, "c_start"),
-    (1, 0, "a_x"), (1, 1, "a_z"), (0, 2, "update"), (1, 0, "s1"), (1, 1, "a_x"), (1, 0, "s2"), (1, 0, "s3"),
-    (1, 2, "a_z"), (1, 1, "s1"), (1, 0, "b_z"), (1, 1, "s2"), (1, 2, "a_x"), (1, 1, "s3"), (1, 0, "b_y"),
-    (1, 2, "s1"), (1, 1, "b_z"), (1, 2, "s2"), (1, 2, "s3"), (1, 0, "c_start"), (1, 1, "b_y"), (1, 2, "b_z"),
-    (1, 0, "update"), (1, 2, "b_y"), (1, 1, "c_start"), (1, 2, "c_start"), (1, 1, "update"), (1, 2, "update"),
+    (0, 0, "a_z"), (0, 1, "a_z"), (0, 0, "a_x"), (0, 1, "a_x"), (0, 0, "s1"), (0, 2, "a_z"), (0, 0, "s2"),
+    (0, 0, "s3"), (0, 1, "s1"), (0, 1, "s2"), (0, 0, "stiff"), (0, 0, "b_z"), (0, 1, "s3"), (0, 2, "a_x"),
+    (0, 0, "b_y"), (0, 1, "b_z"), (0, 2, "s1"), (0, 2, "s2"), (0, 2, "s3"), (0, 1, "b_y"), (0, 0, "c_start"),
+    (0, 2, "b_z"), (0, 0, "update"), (0, 1, "c_start"), (0, 2, "b_y"), (0, 1, "update"), (1, 0, "a_z"),
+    (0, 2, "c_start"), (1, 0, "a_x"), (1, 1, "a_z"), (0, 2, "update"), (1, 0, "s1"), (1, 1, "a_x"), (1, 0, "s2"),
+    (1, 0, "s3"), (1, 2, "a_z"), (1, 1, "s1"), (1, 1, "s2"), (1, 2, "a_x"), (1, 1, "s3"), (1, 0, "b_z"),
+    (1, 2, "s1"), (1, 2, "s2"), (1, 0, "b_y"), (1, 1, "b_z"), (1, 2, "s3"), (1, 1, "b_y"), (1, 2, "b_z"),
+    (1, 0, "c_start"), (1, 2, "b_y"), (1, 1, "c_start"), (1, 0, "update"), (1, 1, "update"), (1, 2, "c_start"),
+    (1, 2, "update"),
 )
 F32 = jnp.float32
 BF16 = jnp.bfloat16
@@ -119,7 +121,7 @@
     disp, resid,
     modulus, faces, w, xs, xr, b1a, b1b, b2a, b2b, zb, fs, fr, zr, ys, yr, corr, rinv,
     cys, cyr, czs, czr, cxs, cxr,
-    send_sem, recv_sem,
+    done, send_sem, recv_sem, out_sem,
 ):
     index = {a: lax.axis_index(a) for a in ("gx", "gy", "gz")}
     count = {a: lax.axis_size(a) for a in ("gx", "gy", "gz")}
@@ -132,7 +134,6 @@
     for a in ("gx", "gy", "gz"):
         pl.semaphore_signal(barrier, inc=1, device_id={a: lower[a]}, device_id_type=MESH)
         pl.semaphore_signal(barrier, inc=1, device_id={a: upper[a]}, device_id_type=MESH)
-    pl.semaphore_wait(barrier, 6)
 
     def copies(slot, phase, down, up):
         a = AXIS[phase]
@@ -158,6 +159,9 @@
         for copy in pending[slot, phase]:
             copy.wait_recv()
 
+    def flat(ref, slot):
+        return ref.at[slot].reshape(PLANES * LENGTH, LANES)
+
     def keep(flag, values):
         return jnp.where(flag, values, 0.0)
 
@@ -171,21 +175,25 @@
             total = jnp.where((lanes == 2 * i) | (lanes == 2 * i + 1), part, total)
         return jnp.transpose(total)[:16]
 
-    def halo_send(slot, values):
+    def y_pack(slot, values):
         cys[slot, 0] = values[:, 0, :]
         cys[slot, 1] = values[:, BRICK - 1, :]
+
+    def y_send(slot):
+        send(slot, CY, (cys.at[slot, 0], cyr.at[slot, 1]), (cys.at[slot, 1], cyr.at[slot, 0]))
+
+    def xz_pack(slot, values):
         czs[slot, 0] = values[0]
         czs[slot, 1] = values[BRICK - 1]
         cxs[slot] = face_columns(values)
-        send(slot, CY, (cys.at[slot, 0], cyr.at[slot, 1]), (cys.at[slot, 1], cyr.at[slot, 0]))
+
+    def xz_send(slot):
         send(slot, CZ, (czs.at[slot, 0], czr.at[slot, 1]), (czs.at[slot, 1], czr.at[slot, 0]))
         send(slot, CX, (cxs.at[slot], cxr.at[slot, 1]), (cxs.at[slot], cxr.at[slot, 0]))
 
-    def halo_get(slot):
-        for phase in (CY, CZ, CX):
+    def halo_get(slot, low_y, high_y):
+        for phase in (CZ, CX):
             arrive(slot, phase)
-        low_y = keep(has_lower["gy"], cyr[slot, 0])
-        high_y = keep(has_upper["gy"], cyr[slot, 1])
         low_z = keep(has_lower["gz"], czr[slot, 0])
         high_z = keep(has_upper["gz"], czr[slot, 1])
         left = keep(has_lower["gx"], cxr[slot, 0])
@@ -208,42 +216,47 @@
         yield jnp.where(lane == 0, side, pltpu.roll(values, 1, 2))
         yield jnp.where(lane == LANES - 1, side, pltpu.roll(values, LANES - 1, 2))
 
-    def a_start(s, c):
+    def a_pack(s, c):
         slot = s * 3 + c
         if s == 0:
             values = load[c]
+            w[slot, 0:BRICK, 0:BRICK, :] = values
         else:
-            values = w[slot, 0:OWNED, :].reshape(BRICK, LENGTH, LANES)
+            values = w[slot, 0:BRICK, 0:BRICK, :]
         ys[slot, 0] = values[:, 0:MARGIN, :]
         ys[slot, 1] = values[:, BRICK - MARGIN:BRICK, :]
+
+    def z_planes(ref, slot, rows):
+        def at(first):
+            return ref.at[slot, pl.ds(first, MARGIN), rows]
+
+        return (at(0), at(BRICK + MARGIN)), (at(BRICK - MARGIN), at(BRICK))
+
+    def a_send(s, c):
+        slot = s * 3 + c
         send(slot, AY, (ys.at[slot, 0], yr.at[slot, 1]), (ys.at[slot, 1], yr.at[slot, 0]))
+        send(slot, AZ, *z_planes(w, slot, pl.ds(0, BRICK)))
 
     def a_z(s, c):
         slot = s * 3 + c
         arrive(slot, AY)
         low = keep(has_lower["gy"], yr[slot, 0])
         high = keep(has_upper["gy"], yr[slot, 1])
-        for z in range(BRICK):
-            w[slot, z * LENGTH + BRICK:(z + 1) * LENGTH, :] = jnp.concatenate([low[z], high[z]], axis=0)
-        first, last = MARGIN * LENGTH, OWNED - MARGIN * LENGTH
-        send(
-            slot, AZ,
-            (w.at[slot, pl.ds(0, first)], w.at[slot, pl.ds(OWNED + first, first)]),
-            (w.at[slot, pl.ds(last, first)], w.at[slot, pl.ds(OWNED, first)]),
-        )
+        w[slot, 0:BRICK, BRICK:LENGTH, :] = jnp.concatenate([low, high], axis=1)
+        send(slot, AE, *z_planes(w, slot, pl.ds(BRICK, 2 * MARGIN)))
 
     def a_x(s, c):
         slot = s * 3 + c
         arrive(slot, AZ)
-        part = MARGIN * LENGTH
-        low = w[slot, OWNED:OWNED + part, :]
-        w[slot, OWNED:OWNED + part, :] = keep(has_lower["gz"], low)
-        high = w[slot, OWNED + part:ROWS, :]
-        w[slot, OWNED + part:ROWS, :] = keep(has_upper["gz"], high)
-
+        arrive(slot, AE)
+        low = w[slot, BRICK:BRICK + MARGIN]
+        w[slot, BRICK:BRICK + MARGIN] = keep(has_lower["gz"], low)
+        high = w[slot, BRICK + MARGIN:LENGTH]
+        w[slot, BRICK + MARGIN:LENGTH] = keep(has_upper["gz"], high)
+        rows = flat(w, slot)
         total = jnp.zeros((LANES, LANES), F32)
         for i in range(CHUNKS):
-            part = pltpu.roll(w[slot, i * LANES:(i + 1) * LANES, :], 8 * i + MARGIN, 1)
+            part = pltpu.roll(rows[i * LANES:(i + 1) * LANES, :], 8 * i + MARGIN, 1)
             total = jnp.where((lanes >= 8 * i) & (lanes < 8 * i + 8), part, total)
         total = jnp.transpose(total)[:CHUNKS * 8].reshape(CHUNKS, 8, LANES)
         xs[slot, 0] = total[:, MARGIN:]
@@ -280,20 +293,21 @@
         slot = s * 3 + c
         arrive(slot, AX)
 
+        rows = flat(w, slot)
         near = jnp.concatenate([keep(has_lower["gx"], xr[slot, 0]), keep(has_upper["gx"], xr[slot, 1])], axis=1)
         high = near.astype(BF16).astype(F32)
         near = jnp.concatenate([high, near - high, high], axis=1)
         sides = []
         for first in range(0, CHUNKS, 5):
-            rows = near[first:first + 5].reshape(-1, LANES)
-            blank = jnp.zeros((LANES - rows.shape[0], LANES), F32)
-            sides.append(jnp.transpose(jnp.concatenate([rows, blank], axis=0)))
+            group = near[first:first + 5].reshape(-1, LANES)
+            blank = jnp.zeros((LANES - group.shape[0], LANES), F32)
+            sides.append(jnp.transpose(jnp.concatenate([group, blank], axis=0)))
         for i in range(CHUNKS):
             at = pl.ds(i * LANES, LANES)
             side = sides[i // 5]
             if i % 5:
                 side = pltpu.roll(side, LANES - 24 * (i % 5), 1)
-            high, low = halves(w[slot, at, :])
+            high, low = halves(rows[at, :])
             out = dot(jnp.concatenate([high, low], axis=1), into_1[...])
             out += dot(jnp.concatenate([high, side.astype(BF16)], axis=1), into_2[...])
             b1a[at, :] = out[:, :LANES]
@@ -309,6 +323,7 @@
         slot = s * 3 + c
         transform(bwd, two, one, False)
 
+        rows = flat(zb, slot)
         margin = jnp.zeros((LANES, LANES), F32)
         for i in range(CHUNKS):
             at = pl.ds(i * LANES, LANES)
@@ -318,7 +333,7 @@
             packed = tail_high + pltpu.roll(tail - tail_high, 32, 1) + pltpu.roll(tail_high, 64, 1)
             out = dot(jnp.concatenate([high, low], axis=1), out_1[...])
             out += dot(jnp.concatenate([high, packed.astype(BF16)], axis=1), out_2[...])
-            zb[slot, at, :] = out[:, :LANES]
+            rows[at, :] = out[:, :LANES]
             part = out[:, LANES:]
             margin += pltpu.roll(part, 8 * i, 1) if i else part
         margin = jnp.transpose(margin)[:CHUNKS * 8].reshape(CHUNKS, 8, LANES)
@@ -333,38 +348,38 @@
         near = jnp.concatenate([keep(has_upper["gx"], fr[slot, 1]), keep(has_lower["gx"], fr[slot, 0])], axis=1)
         blank = jnp.zeros((LANES - CHUNKS * 8, LANES), F32)
         side = jnp.transpose(jnp.concatenate([near.reshape(CHUNKS * 8, LANES), blank], axis=0))
+        rows = flat(zb, slot)
         edge = (lanes < MARGIN) | (lanes >= LANES - MARGIN)
         for i in range(CHUNKS):
             at = pl.ds(i * LANES, LANES)
-            zb[slot, at, :] += jnp.where(edge, pltpu.roll(side, LANES - 8 * i - MARGIN, 1), 0.0)
-
-        part = MARGIN * LENGTH
+            rows[at, :] += jnp.where(edge, pltpu.roll(side, LANES - 8 * i - MARGIN, 1), 0.0)
+
         send(
             slot, BZ,
-            (zb.at[slot, pl.ds(OWNED, part)], zr.at[slot, 1]),
-            (zb.at[slot, pl.ds(OWNED + part, part)], zr.at[slot, 0]),
+            (zb.at[slot, pl.ds(BRICK, MARGIN)], zr.at[slot, 1]),
+            (zb.at[slot, pl.ds(BRICK + MARGIN, MARGIN)], zr.at[slot, 0]),
         )
 
     def b_y(s, c):
         slot = s * 3 + c
         arrive(slot, BZ)
-        part = MARGIN * LENGTH
-        zb[slot, 0:part, :] += keep(has_lower["gz"], zr[slot, 0])
-        zb[slot, OWNED - part:OWNED, :] += keep(has_upper["gz"], zr[slot, 1])
-        other = slot + 6
-        for z in range(BRICK):
-            rows = zb[slot, z * LENGTH + BRICK:(z + 1) * LENGTH, :]
-            ys[other, 0, z] = rows[:MARGIN]
-            ys[other, 1, z] = rows[MARGIN:]
+        zb[slot, 0:MARGIN] += keep(has_lower["gz"], zr[slot, 0])
+        zb[slot, BRICK - MARGIN:BRICK] += keep(has_upper["gz"], zr[slot, 1])
+        other = slot + 3 * SWEEPS
+        rows = zb[slot, 0:BRICK, BRICK:LENGTH, :]
+        ys[other, 0] = rows[:, :MARGIN]
+        ys[other, 1] = rows[:, MARGIN:]
+        y_pack(slot, zb[slot, 0:BRICK, 0:BRICK, :])
         send(slot, BY, (ys.at[other, 0], yr.at[other, 1]), (ys.at[other, 1], yr.at[other, 0]))
+        y_send(slot)
 
     def c_start(s, c):
         slot = s * 3 + c
         arrive(slot, BY)
-        other = slot + 6
+        other = slot + 3 * SWEEPS
         low = keep(has_lower["gy"], yr[other, 0])
         high = keep(has_upper["gy"], yr[other, 1])
-        own = zb[slot, 0:OWNED, :].reshape(BRICK, LENGTH, LANES)[:, :BRICK]
+        own = zb[slot, 0:BRICK, 0:BRICK, :]
         blank = jnp.zeros((BRICK, MARGIN, LANES), F32)
         own = jnp.concatenate([
             own[:, :8] + jnp.concatenate([low, blank], axis=1),
@@ -372,37 +387,54 @@
             own[:, 24:] + jnp.concatenate([blank, high], axis=1),
         ], axis=1)
         corr[slot] = own
-        halo_send(slot, own)
-        if s == 0:
-            disp[c] = own
-        else:
-            disp[c] += own
+        xz_pack(slot, own)
+        xz_send(slot)
+        if s == SWEEPS - 1:
+            total = own
+            for before in range(s):
+                total = corr[before * 3 + c] + total
+            done[0, c] = total
+            store(0, c, disp)
+
+    def store(which, c, target):
+        copy = pltpu.make_async_copy(done.at[which, c], target.at[c], out_sem.at[which * 3 + c])
+        copy.start()
+        stores.append(copy)
+
+    stores = []
 
     def update(s, c):
         slot = s * 3 + c
-        halo = halo_get(slot)
+        arrive(slot, CY)
+        margins = zb[slot, 0:BRICK, BRICK:LENGTH, :]
+        halo = halo_get(
+            slot,
+            keep(has_lower["gy"], cyr[slot, 0] + margins[:, MARGIN - 1, :]),
+            keep(has_upper["gy"], cyr[slot, 1] + margins[:, MARGIN, :]),
+        )
         values = corr[slot]
         total = SIGMA_SHIFT * modulus[...] * values
         for number, moved in enumerate(shifts(values, halo)):
             total = total + (ratio(c, number // 2) * 0.5) * faces[number] * (values - moved)
-        if s == 0:
-            old = load[c]
+        if s == SWEEPS - 1:
+            done[1, c] = w[slot, 0:BRICK, 0:BRICK, :] - total
+            store(1, c, resid)
         else:
-            old = w[slot, 0:OWNED, :].reshape(BRICK, LENGTH, LANES)[:, :BRICK]
-        new = old - total
-        if s == SWEEPS - 1:
-            resid[c] = new
-        else:
-            for z in range(BRICK):
-                w[slot + 3, z * LENGTH:z * LENGTH + BRICK, :] = new[z]
+            w[slot + 3, 0:BRICK, 0:BRICK, :] = w[slot, 0:BRICK, 0:BRICK, :] - total
+            a_pack(s + 1, c)
+            a_send(s + 1, c)
+
+    def stiff(s, c):
+        arrive(6, CY)
+        own = modulus[...]
+        low, high = keep(has_lower["gy"], cyr[6, 0]), keep(has_upper["gy"], cyr[6, 1])
+        for number, moved in enumerate(shifts(own, halo_get(6, low, high))):
+            faces[number] = own + moved
 
     for c in range(3):
-        a_start(0, c)
-    for c in range(3):
-        for z in range(BRICK):
-            w[c, z * LENGTH:z * LENGTH + BRICK, :] = load[c, z]
+        a_pack(0, c)
     for slot in range(6):
-        w[slot, ROWS:, :] = jnp.zeros((PADDED - ROWS, LANES), F32)
+        w[slot, LENGTH:] = jnp.zeros((PLANES - LENGTH, LENGTH, LANES), F32)
 
     def look(z, carry):
         picked = labels[z]
@@ -413,7 +445,8 @@
         return carry
 
     lax.fori_loop(0, BRICK, look, 0)
-    halo_send(6, modulus[...])
+    y_pack(6, modulus[...])
+    xz_pack(6, modulus[...])
 
     for c in range(3):
         def invert(y, carry, c=c):
@@ -428,19 +461,22 @@
 
         lax.fori_loop(0, LENGTH, invert, 0)
 
-    own = modulus[...]
-    for number, moved in enumerate(shifts(own, halo_get(6))):
-        faces[number] = own + moved
-
-    stages = dict(a_z=a_z, a_x=a_x, s1=s1, s2=s2, s3=s3, b_z=b_z, b_y=b_y, c_start=c_start, update=update)
+    pl.semaphore_wait(barrier, 6)
+    for c in range(3):
+        a_send(0, c)
+    y_send(6)
+    xz_send(6)
+
+    stages = dict(a_z=a_z, a_x=a_x, s1=s1, s2=s2, s3=s3, b_z=b_z, b_y=b_y, c_start=c_start, update=update,
+                  stiff=stiff)
     for s, c, name in ORDER:
         stages[name](s, c)
-        if name == "update" and s < SWEEPS - 1:
-            a_start(s + 1, c)
 
     for made in pending.values():
         for copy in made:
             copy.wait_send()
+    for copy in stores:
+        copy.wait()
 
 
 def local(load, labels, mask, table):
@@ -454,21 +490,21 @@
         kernel,
         out_shape=(field, field),
         in_specs=[vmem, vmem, vmem, smem] + [vmem] * len(tables),
-        out_specs=(vmem, vmem),
+        out_specs=(pl.BlockSpec(memory_space=pl.ANY),) * 2,
         scratch_shapes=[
             pltpu.VMEM(block, F32),
             pltpu.VMEM((6,) + block, F32),
-            pltpu.VMEM((slots, PADDED, LANES), F32),
+            pltpu.VMEM((slots, PLANES, LENGTH, LANES), F32),
             pltpu.VMEM((slots, 2, CHUNKS, MARGIN, LANES), F32),
             pltpu.VMEM((slots, 2, CHUNKS, MARGIN, LANES), F32),
             pltpu.VMEM((PADDED, LANES), F32),
             pltpu.VMEM((PADDED, LANES), F32),
             pltpu.VMEM((PADDED, LANES), F32),
             pltpu.VMEM((PADDED, LANES), F32),
-            pltpu.VMEM((slots, PADDED, LANES), F32),
+            pltpu.VMEM((slots, PLANES, LENGTH, LANES), F32),
             pltpu.VMEM((slots, 2, CHUNKS, MARGIN, LANES), F32),
             pltpu.VMEM((slots, 2, CHUNKS, MARGIN, LANES), F32),
-            pltpu.VMEM((slots, 2, MARGIN * LENGTH, LANES), F32),
+            pltpu.VMEM((slots, 2, MARGIN, LENGTH, LANES), F32),
             pltpu.VMEM((2 * slots, 2, BRICK, MARGIN, LANES), F32),
             pltpu.VMEM((2 * slots, 2, BRICK, MARGIN, LANES), F32),
             pltpu.VMEM((slots,) + block, F32),
@@ -479,8 +515,10 @@
             pltpu.VMEM((slots + 1, 2, BRICK, LANES), F32),
             pltpu.VMEM((slots + 1, 16, LANES), F32),
             pltpu.VMEM((slots + 1, 2, 16, LANES), F32),
+            pltpu.VMEM((2, 3) + block, F32),
             pltpu.SemaphoreType.DMA(((slots + 1) * PHASES * 2,)),
             pltpu.SemaphoreType.DMA(((slots + 1) * PHASES * 2,)),
+            pltpu.SemaphoreType.DMA((6,)),
         ],
         compiler_params=pltpu.CompilerParams(
             collective_id=0, has_side_effects=True, vmem_limit_bytes=62 * 1024 * 1024

time: 119 us -> 112 us (0.941)
  Pallas kernels: 114 us -> 107 us
    pallas_call x1, Pallas kernels: 114 us -> 107 us  [local(): pl.pallas_call(kernel, out_shape=(field, field), in_specs=[vmem, vmem, vm...]
where the time goes in v4:
time: 112 us; the launch traced here: 111 us
  Pallas kernels  107 us (96%)
  local copies, waits for them, and re-layouts  3.93 us (4%)
    pallas_call x1, Pallas kernels, local(): pl.pallas_call(kernel, out_shape=(field, field), in_specs=[vmem, vmem, vm...  107 us
    unnamed x4, local copies, waits for them, and re-layouts  3.93 us

profile of v4, /device:TPU:1, one launch (start us, length us, event | category | flops | bytes accessed | tf_op | source)
XLA Modules:
  0.0 111.5 jit_solution(877909349760847890)
XLA Ops:
  0.6 106.9 %shard_map.131 = (f32[3,32,32,128]{3,2,1,0:T(8,128)}, f32[3,32,32,128]{3,2,1,0:T(8,128)}) custom-call(f32[3,32,32,128]{3,2,1,0:T(8,128)} %load.1, s32[32,32,128]{2,1,0:T(8,128)} %labels.1, s32[32,32,128]{2,1,0:T(8,128)} %mask.1, f32[16]{0:T(128)} %table.1, bf16[80,240]{1,0:T(8,128)(2,1)} %constant.16.clone.fwd, bf16[80,240]{1,0:T(8,128)(2,1)} %constant.17.clone.bwd, ...), custom_call_target="tpu_custom_call" | custom-call | tf_op jit(solution)/shard_map/pallas_call | solution.py:489
  107.6 0.0 copy-start
  107.6 2.8 %copy.16 = f32[3,32,32,128]{3,2,1,0:T(8,128)} copy(f32[3,32,32,128]{3,2,1,0:T(8,128)} %get-tuple-element.4) | data formatting | bytes 3145728
  110.3 0.0 copy-done
  110.4 1.1 %copy.17 = f32[3,32,32,128]{3,2,1,0:T(8,128)} copy(f32[3,32,32,128]{3,2,1,0:T(8,128)S(1)} %copy-done) | data formatting | bytes 3145728
Async XLA Ops:
  107.6 2.8 %copy-start = (f32[3,32,32,128]{3,2,1,0:T(8,128)S(1)}, f32[3,32,32,128]{3,2,1,0:T(8,128)}, u32[]{:S(2)}) copy-start(f32[3,32,32,128]{3,2,1,0:T(8,128)} %get-tuple-element.5) | copy-start | bytes 4718596

commit v5 on v4

--- a/solution.py
+++ b/solution.py
@@ -22,20 +22,19 @@
 VOID_MODULUS = 0.1
 MESH = pl.DeviceIdType.MESH
 UNROLL = 5
-PHASES = 10
-AY, AZ, AE, AX, BX, BZ, BY, CY, CZ, CX = range(PHASES)
-AXIS = ("gy", "gz", "gz", "gx", "gx", "gz", "gy", "gy", "gz", "gx")
+PHASES = 9
+AY, AZ, AX, BX, BZ, BY, CY, CZ, CX = range(PHASES)
+AXIS = ("gy", "gz", "gx", "gx", "gz", "gy", "gy", "gz", "gx")
+QUARTERS = ((0, 0), (0, 1), (1, 0), (1, 1))
 PLANES = 42
 ORDER = (
-    (0, 0, "a_z"), (0, 1, "a_z"), (0, 0, "a_x"), (0, 1, "a_x"), (0, 0, "s1"), (0, 2, "a_z"), (0, 0, "s2"),
-    (0, 0, "s3"), (0, 1, "s1"), (0, 1, "s2"), (0, 0, "stiff"), (0, 0, "b_z"), (0, 1, "s3"), (0, 2, "a_x"),
-    (0, 0, "b_y"), (0, 1, "b_z"), (0, 2, "s1"), (0, 2, "s2"), (0, 2, "s3"), (0, 1, "b_y"), (0, 0, "c_start"),
-    (0, 2, "b_z"), (0, 0, "update"), (0, 1, "c_start"), (0, 2, "b_y"), (0, 1, "update"), (1, 0, "a_z"),
-    (0, 2, "c_start"), (1, 0, "a_x"), (1, 1, "a_z"), (0, 2, "update"), (1, 0, "s1"), (1, 1, "a_x"), (1, 0, "s2"),
-    (1, 0, "s3"), (1, 2, "a_z"), (1, 1, "s1"), (1, 1, "s2"), (1, 2, "a_x"), (1, 1, "s3"), (1, 0, "b_z"),
-    (1, 2, "s1"), (1, 2, "s2"), (1, 0, "b_y"), (1, 1, "b_z"), (1, 2, "s3"), (1, 1, "b_y"), (1, 2, "b_z"),
-    (1, 0, "c_start"), (1, 2, "b_y"), (1, 1, "c_start"), (1, 0, "update"), (1, 1, "update"), (1, 2, "c_start"),
-    (1, 2, "update"),
+    (0, 0, "a_x"), (0, 1, "a_x"), (0, 0, "s1"), (0, 0, "s2"), (0, 2, "a_x"), (0, 0, "s3"), (0, 1, "s1"),
+    (0, 1, "s2"), (0, 0, "stiff"), (0, 0, "b_x"), (0, 1, "s3"), (0, 2, "s1"), (0, 2, "s2"), (0, 1, "b_x"),
+    (0, 2, "s3"), (0, 0, "c_start"), (0, 2, "b_x"), (0, 0, "update"), (0, 1, "c_start"), (0, 1, "update"),
+    (0, 2, "c_start"), (1, 0, "a_x"), (0, 2, "update"), (1, 1, "a_x"), (1, 0, "s1"), (1, 0, "s2"), (1, 0, "s3"),
+    (1, 2, "a_x"), (1, 1, "s1"), (1, 1, "s2"), (1, 0, "b_x"), (1, 1, "s3"), (1, 2, "s1"), (1, 2, "s2"),
+    (1, 1, "b_x"), (1, 2, "s3"), (1, 0, "c_start"), (1, 2, "b_x"), (1, 0, "update"), (1, 1, "c_start"),
+    (1, 1, "update"), (1, 2, "c_start"), (1, 2, "update"),
 )
 F32 = jnp.float32
 BF16 = jnp.bfloat16
@@ -121,7 +120,7 @@
     disp, resid,
     modulus, faces, w, xs, xr, b1a, b1b, b2a, b2b, zb, fs, fr, zr, ys, yr, corr, rinv,
     cys, cyr, czs, czr, cxs, cxr,
-    done, send_sem, recv_sem, out_sem,
+    de, dr, send_sem, recv_sem, corner_send, corner_recv,
 ):
     index = {a: lax.axis_index(a) for a in ("gx", "gy", "gz")}
     count = {a: lax.axis_size(a) for a in ("gx", "gy", "gz")}
@@ -134,6 +133,11 @@
     for a in ("gx", "gy", "gz"):
         pl.semaphore_signal(barrier, inc=1, device_id={a: lower[a]}, device_id_type=MESH)
         pl.semaphore_signal(barrier, inc=1, device_id={a: upper[a]}, device_id_type=MESH)
+    near = (lower, upper)
+    for z, y in QUARTERS:
+        pl.semaphore_signal(
+            barrier, inc=1, device_id={"gz": near[z]["gz"], "gy": near[y]["gy"]}, device_id_type=MESH
+        )
 
     def copies(slot, phase, down, up):
         a = AXIS[phase]
@@ -158,6 +162,28 @@
     def arrive(slot, phase):
         for copy in pending[slot, phase]:
             copy.wait_recv()
+
+    def send_corners(slot, sources, size):
+        made = []
+        for quarter, (z, y) in enumerate(QUARTERS):
+            number = slot * 4 + quarter
+            made.append(pltpu.make_async_remote_copy(
+                src_ref=sources[quarter], dst_ref=dr.at[slot, 3 - quarter, pl.ds(0, size)],
+                send_sem=corner_send.at[number], recv_sem=corner_recv.at[slot * 4 + 3 - quarter],
+                device_id={"gz": near[z]["gz"], "gy": near[y]["gy"]}, device_id_type=MESH,
+            ))
+        for copy in made:
+            copy.start()
+        pending[slot, "corner"] = made
+
+    def arrive_corners(slot, size):
+        blocks = []
+        for copy in reversed(pending[slot, "corner"]):
+            copy.wait_recv()
+        for quarter, (z, y) in enumerate(QUARTERS):
+            flag = (has_lower, has_upper)[z]["gz"] & (has_lower, has_upper)[y]["gy"]
+            blocks.append(keep(flag, dr[slot, quarter, 0:size]))
+        return blocks
 
     def flat(ref, slot):
         return ref.at[slot].reshape(PLANES * LENGTH, LANES)
@@ -226,33 +252,30 @@
         ys[slot, 0] = values[:, 0:MARGIN, :]
         ys[slot, 1] = values[:, BRICK - MARGIN:BRICK, :]
 
-    def z_planes(ref, slot, rows):
-        def at(first):
-            return ref.at[slot, pl.ds(first, MARGIN), rows]
-
-        return (at(0), at(BRICK + MARGIN)), (at(BRICK - MARGIN), at(BRICK))
-
     def a_send(s, c):
         slot = s * 3 + c
+        ends = (pl.ds(0, MARGIN), pl.ds(BRICK - MARGIN, MARGIN))
+        send_corners(slot, [ys.at[slot, y, ends[z]] for z, y in QUARTERS], MARGIN)
         send(slot, AY, (ys.at[slot, 0], yr.at[slot, 1]), (ys.at[slot, 1], yr.at[slot, 0]))
-        send(slot, AZ, *z_planes(w, slot, pl.ds(0, BRICK)))
-
-    def a_z(s, c):
+        own = pl.ds(0, BRICK)
+        send(
+            slot, AZ,
+            (w.at[slot, ends[0], own], w.at[slot, pl.ds(BRICK + MARGIN, MARGIN), own]),
+            (w.at[slot, ends[1], own], w.at[slot, pl.ds(BRICK, MARGIN), own]),
+        )
+
+    def a_x(s, c):
         slot = s * 3 + c
         arrive(slot, AY)
         low = keep(has_lower["gy"], yr[slot, 0])
         high = keep(has_upper["gy"], yr[slot, 1])
         w[slot, 0:BRICK, BRICK:LENGTH, :] = jnp.concatenate([low, high], axis=1)
-        send(slot, AE, *z_planes(w, slot, pl.ds(BRICK, 2 * MARGIN)))
-
-    def a_x(s, c):
-        slot = s * 3 + c
+        blocks = arrive_corners(slot, MARGIN)
         arrive(slot, AZ)
-        arrive(slot, AE)
-        low = w[slot, BRICK:BRICK + MARGIN]
-        w[slot, BRICK:BRICK + MARGIN] = keep(has_lower["gz"], low)
-        high = w[slot, BRICK + MARGIN:LENGTH]
-        w[slot, BRICK + MARGIN:LENGTH] = keep(has_upper["gz"], high)
+        for z, flag in ((0, has_lower["gz"]), (1, has_upper["gz"])):
+            planes = slice(BRICK + z * MARGIN, BRICK + (z + 1) * MARGIN)
+            w[slot, planes, 0:BRICK, :] = keep(flag, w[slot, planes, 0:BRICK, :])
+            w[slot, planes, BRICK:LENGTH, :] = jnp.concatenate([blocks[2 * z], blocks[2 * z + 1]], axis=1)
         rows = flat(w, slot)
         total = jnp.zeros((LANES, LANES), F32)
         for i in range(CHUNKS):
@@ -341,7 +364,7 @@
         fs[slot, 1] = margin[:, MARGIN:]
         send(slot, BX, (fs.at[slot, 0], fr.at[slot, 1]), (fs.at[slot, 1], fr.at[slot, 0]))
 
-    def b_z(s, c):
+    def b_x(s, c):
         slot = s * 3 + c
         arrive(slot, BX)
 
@@ -354,31 +377,50 @@
             at = pl.ds(i * LANES, LANES)
             rows[at, :] += jnp.where(edge, pltpu.roll(side, LANES - 8 * i - MARGIN, 1), 0.0)
 
+        other = slot + 3 * SWEEPS
+        rows = zb[slot, :LENGTH, BRICK:LENGTH, :]
+        values = zb[slot, :LENGTH, 0:BRICK, :]
+        for quarter, (z, y) in enumerate(QUARTERS):
+            planes = slice(BRICK + z * MARGIN, BRICK + (z + 1) * MARGIN)
+            de[slot, quarter, 0:MARGIN] = rows[planes, y * MARGIN:(y + 1) * MARGIN]
+            de[slot, quarter, MARGIN] = values[planes, y * (BRICK - 1)]
+        ys[other, 0] = rows[:BRICK, :MARGIN]
+        ys[other, 1] = rows[:BRICK, MARGIN:]
+        y_pack(slot, values[:BRICK])
+        send_corners(other, [de.at[slot, quarter] for quarter in range(4)], MARGIN + 1)
+        send(slot, BY, (ys.at[other, 0], yr.at[other, 1]), (ys.at[other, 1], yr.at[other, 0]))
+        y_send(slot)
         send(
             slot, BZ,
             (zb.at[slot, pl.ds(BRICK, MARGIN)], zr.at[slot, 1]),
             (zb.at[slot, pl.ds(BRICK + MARGIN, MARGIN)], zr.at[slot, 0]),
         )
 
-    def b_y(s, c):
-        slot = s * 3 + c
+    def c_start(s, c):
+        slot = s * 3 + c
+        other = slot + 3 * SWEEPS
         arrive(slot, BZ)
         zb[slot, 0:MARGIN] += keep(has_lower["gz"], zr[slot, 0])
         zb[slot, BRICK - MARGIN:BRICK] += keep(has_upper["gz"], zr[slot, 1])
-        other = slot + 3 * SWEEPS
-        rows = zb[slot, 0:BRICK, BRICK:LENGTH, :]
-        ys[other, 0] = rows[:, :MARGIN]
-        ys[other, 1] = rows[:, MARGIN:]
-        y_pack(slot, zb[slot, 0:BRICK, 0:BRICK, :])
-        send(slot, BY, (ys.at[other, 0], yr.at[other, 1]), (ys.at[other, 1], yr.at[other, 0]))
-        y_send(slot)
-
-    def c_start(s, c):
-        slot = s * 3 + c
         arrive(slot, BY)
-        other = slot + 3 * SWEEPS
-        low = keep(has_lower["gy"], yr[other, 0])
-        high = keep(has_upper["gy"], yr[other, 1])
+        arrive(slot, CY)
+        blocks = arrive_corners(other, MARGIN + 1)
+        margins = zb[slot, 0:BRICK, BRICK:LENGTH, :]
+
+        def joined(y, flag):
+            near, far = blocks[y], blocks[2 + y]
+            rows = keep(flag, yr[other, y])
+            rows = jnp.concatenate([
+                rows[:MARGIN] + near[:MARGIN], rows[MARGIN:BRICK - MARGIN], rows[BRICK - MARGIN:] + far[:MARGIN]
+            ], axis=0)
+            face = keep(flag, cyr[slot, y] + margins[:, MARGIN - 1 + y, :])
+            blank = jnp.zeros((BRICK - 2 * MARGIN, LANES), F32)
+            return rows, face + jnp.concatenate([near[MARGIN], blank, far[MARGIN]], axis=0)
+
+        low, face = joined(0, has_lower["gy"])
+        cyr[slot, 0] = face
+        high, face = joined(1, has_upper["gy"])
+        cyr[slot, 1] = face
         own = zb[slot, 0:BRICK, 0:BRICK, :]
         blank = jnp.zeros((BRICK, MARGIN, LANES), F32)
         own = jnp.concatenate([
@@ -393,32 +435,17 @@
             total = own
             for before in range(s):
                 total = corr[before * 3 + c] + total
-            done[0, c] = total
-            store(0, c, disp)
-
-    def store(which, c, target):
-        copy = pltpu.make_async_copy(done.at[which, c], target.at[c], out_sem.at[which * 3 + c])
-        copy.start()
-        stores.append(copy)
-
-    stores = []
+            disp[c] = total
 
     def update(s, c):
         slot = s * 3 + c
-        arrive(slot, CY)
-        margins = zb[slot, 0:BRICK, BRICK:LENGTH, :]
-        halo = halo_get(
-            slot,
-            keep(has_lower["gy"], cyr[slot, 0] + margins[:, MARGIN - 1, :]),
-            keep(has_upper["gy"], cyr[slot, 1] + margins[:, MARGIN, :]),
-        )
+        halo = halo_get(slot, cyr[slot, 0], cyr[slot, 1])
         values = corr[slot]
         total = SIGMA_SHIFT * modulus[...] * values
         for number, moved in enumerate(shifts(values, halo)):
             total = total + (ratio(c, number // 2) * 0.5) * faces[number] * (values - moved)
         if s == SWEEPS - 1:
-            done[1, c] = w[slot, 0:BRICK, 0:BRICK, :] - total
-            store(1, c, resid)
+            resid[c] = w[slot, 0:BRICK, 0:BRICK, :] - total
         else:
             w[slot + 3, 0:BRICK, 0:BRICK, :] = w[slot, 0:BRICK, 0:BRICK, :] - total
             a_pack(s + 1, c)
@@ -461,13 +488,13 @@
 
         lax.fori_loop(0, LENGTH, invert, 0)
 
-    pl.semaphore_wait(barrier, 6)
+    pl.semaphore_wait(barrier, 10)
     for c in range(3):
         a_send(0, c)
     y_send(6)
     xz_send(6)
 
-    stages = dict(a_z=a_z, a_x=a_x, s1=s1, s2=s2, s3=s3, b_z=b_z, b_y=b_y, c_start=c_start, update=update,
+    stages = dict(a_x=a_x, s1=s1, s2=s2, s3=s3, b_x=b_x, c_start=c_start, update=update,
                   stiff=stiff)
     for s, c, name in ORDER:
         stages[name](s, c)
@@ -475,8 +502,6 @@
     for made in pending.values():
         for copy in made:
             copy.wait_send()
-    for copy in stores:
-        copy.wait()
 
 
 def local(load, labels, mask, table):
@@ -490,7 +515,7 @@
         kernel,
         out_shape=(field, field),
         in_specs=[vmem, vmem, vmem, smem] + [vmem] * len(tables),
-        out_specs=(pl.BlockSpec(memory_space=pl.ANY),) * 2,
+        out_specs=(vmem, vmem),
         scratch_shapes=[
             pltpu.VMEM(block, F32),
             pltpu.VMEM((6,) + block, F32),
@@ -515,13 +540,15 @@
             pltpu.VMEM((slots + 1, 2, BRICK, LANES), F32),
             pltpu.VMEM((slots + 1, 16, LANES), F32),
             pltpu.VMEM((slots + 1, 2, 16, LANES), F32),
-            pltpu.VMEM((2, 3) + block, F32),
+            pltpu.VMEM((slots, 4, MARGIN + 1, MARGIN, LANES), F32),
+            pltpu.VMEM((2 * slots, 4, MARGIN + 1, MARGIN, LANES), F32),
             pltpu.SemaphoreType.DMA(((slots + 1) * PHASES * 2,)),
             pltpu.SemaphoreType.DMA(((slots + 1) * PHASES * 2,)),
-            pltpu.SemaphoreType.DMA((6,)),
+            pltpu.SemaphoreType.DMA((2 * slots * 4,)),
+            pltpu.SemaphoreType.DMA((2 * slots * 4,)),
         ],
         compiler_params=pltpu.CompilerParams(
-            collective_id=0, has_side_effects=True, vmem_limit_bytes=62 * 1024 * 1024
+            collective_id=0, has_side_effects=True, vmem_limit_bytes=36 * 1024 * 1024
         ),
     )(load, labels, mask, table, *tables)
 

time: 112 us -> 120 us (1.071)
  local copies, waits for them, and re-layouts: 3.93 us -> 13.1 us
    unnamed x4 -> x26, local copies, waits for them, and re-layouts: 3.93 us -> 13.1 us
where the time goes in v5:
time: 120 us; the launch traced here: 119 us
  Pallas kernels  106 us (88%)
  local copies, waits for them, and re-layouts  13.1 us (11%)
    pallas_call x1, Pallas kernels, local(): pl.pallas_call(kernel, out_shape=(field, field), in_specs=[vmem, vmem, vm...  106 us
    unnamed x26, local copies, waits for them, and re-layouts  13.1 us

profile of v5, /device:TPU:1, one launch (start us, length us, event | category | flops | bytes accessed | tf_op | source)
XLA Modules:
  0.0 119.4 jit_solution(7581676326310240463)
XLA Ops:
  0.6 0.0 copy-start
  0.6 1.4 %copy-done = f32[3,32,32,128]{3,2,1,0:T(8,128)S(1)} copy-done((f32[3,32,32,128]{3,2,1,0:T(8,128)S(1)}, f32[3,32,32,128]{3,2,1,0:T(8,128)}, u32[]{:S(2)}) %copy-start) | copy-done | bytes 1572888
  2.0 0.0 copy-start.1
  2.0 1.0 copy-done.1
  3.1 0.0 copy-start.2
  3.1 1.0 copy-done.2
  4.1 0.0 copy-start.3
  4.1 0.9 copy-done.3
  5.0 0.0 copy-start.4
  5.0 0.9 copy-done.4
  5.9 0.0 copy-start.5
  5.9 0.9 copy-done.5
  6.8 0.0 copy-start.6
  6.8 0.9 copy-done.6
  7.7 0.0 copy-start.7
  7.7 0.8 copy-done.7
  8.5 0.0 copy-start.8
  8.5 0.8 copy-done.8
  9.3 0.8 copy-done.9
  10.1 0.7 copy-done.10
  10.8 0.7 copy-done.11
  11.4 105.7 %shard_map.131 = (f32[3,32,32,128]{3,2,1,0:T(8,128)S(1)}, f32[3,32,32,128]{3,2,1,0:T(8,128)S(1)}) custom-call(f32[3,32,32,128]{3,2,1,0:T(8,128)S(1)} %copy-done, s32[32,32,128]{2,1,0:T(8,128)S(1)} %copy-done.1, s32[32,32,128]{2,1,0:T(8,128)S(1)} %copy-done.2, f32[16]{0:T(128)S(1)} %copy-done.11, bf16[80,240]{1,0:T(8,128)(2,1)S(1)} %copy-done.9, ...), custom_call_target="tpu_custom_call" | custom-call | tf_op jit(solution)/shard_map/pallas_call | solution.py:514
  117.2 1.1 copy.16
  118.3 1.1 copy.17
  (3 shorter events, 0.0 us)
Async XLA Ops:
  0.6 1.4 %copy-start = (f32[3,32,32,128]{3,2,1,0:T(8,128)S(1)}, f32[3,32,32,128]{3,2,1,0:T(8,128)}, u32[]{:S(2)}) copy-start(f32[3,32,32,128]{3,2,1,0:T(8,128)} %load.1) | copy-start | bytes 4718596
  2.0 1.0 copy-start.1
  3.1 1.0 copy-start.2
  4.1 0.9 copy-start.3
  5.0 0.9 copy-start.4
  5.9 0.9 copy-start.5
  6.8 0.9 copy-start.6
  7.7 0.8 copy-start.7
  8.5 0.8 copy-start.8
  9.3 0.8 copy-start.9
  10.1 0.7 copy-start.10
  10.8 0.7 copy-start.11

commit v6 on v4

--- a/solution.py
+++ b/solution.py
@@ -26,15 +26,16 @@
 AY, AZ, AE, AX, BX, BZ, BY, CY, CZ, CX = range(PHASES)
 AXIS = ("gy", "gz", "gz", "gx", "gx", "gz", "gy", "gy", "gz", "gx")
 PLANES = 42
+TABLES = 8
 ORDER = (
-    (0, 0, "a_z"), (0, 1, "a_z"), (0, 0, "a_x"), (0, 1, "a_x"), (0, 0, "s1"), (0, 2, "a_z"), (0, 0, "s2"),
-    (0, 0, "s3"), (0, 1, "s1"), (0, 1, "s2"), (0, 0, "stiff"), (0, 0, "b_z"), (0, 1, "s3"), (0, 2, "a_x"),
-    (0, 0, "b_y"), (0, 1, "b_z"), (0, 2, "s1"), (0, 2, "s2"), (0, 2, "s3"), (0, 1, "b_y"), (0, 0, "c_start"),
-    (0, 2, "b_z"), (0, 0, "update"), (0, 1, "c_start"), (0, 2, "b_y"), (0, 1, "update"), (1, 0, "a_z"),
-    (0, 2, "c_start"), (1, 0, "a_x"), (1, 1, "a_z"), (0, 2, "update"), (1, 0, "s1"), (1, 1, "a_x"), (1, 0, "s2"),
-    (1, 0, "s3"), (1, 2, "a_z"), (1, 1, "s1"), (1, 1, "s2"), (1, 2, "a_x"), (1, 1, "s3"), (1, 0, "b_z"),
-    (1, 2, "s1"), (1, 2, "s2"), (1, 0, "b_y"), (1, 1, "b_z"), (1, 2, "s3"), (1, 1, "b_y"), (1, 2, "b_z"),
-    (1, 0, "c_start"), (1, 2, "b_y"), (1, 1, "c_start"), (1, 0, "update"), (1, 1, "update"), (1, 2, "c_start"),
+    (0, 0, "a_z"), (0, 1, "a_z"), (0, 0, "a_x"), (0, 2, "a_z"), (0, 1, "a_x"), (0, 0, "s1"), (0, 0, "s2"),
+    (0, 0, "s3"), (0, 1, "s1"), (0, 2, "a_x"), (0, 0, "stiff"), (0, 0, "b_z"), (0, 1, "s2"), (0, 1, "s3"),
+    (0, 0, "b_y"), (0, 2, "s1"), (0, 1, "b_z"), (0, 2, "s2"), (0, 2, "s3"), (0, 0, "c_start"), (0, 1, "b_y"),
+    (0, 2, "b_z"), (0, 0, "update"), (0, 1, "c_start"), (0, 2, "b_y"), (1, 0, "a_z"), (0, 1, "update"),
+    (1, 0, "a_x"), (0, 2, "c_start"), (1, 1, "a_z"), (0, 2, "update"), (1, 0, "s1"), (1, 1, "a_x"), (1, 0, "s2"),
+    (1, 0, "s3"), (1, 2, "a_z"), (1, 1, "s1"), (1, 1, "s2"), (1, 2, "a_x"), (1, 0, "b_z"), (1, 1, "s3"),
+    (1, 2, "s1"), (1, 2, "s2"), (1, 1, "b_z"), (1, 2, "s3"), (1, 0, "b_y"), (1, 2, "b_z"), (1, 1, "b_y"),
+    (1, 2, "b_y"), (1, 0, "c_start"), (1, 1, "c_start"), (1, 2, "c_start"), (1, 0, "update"), (1, 1, "update"),
     (1, 2, "update"),
 )
 F32 = jnp.float32
@@ -116,13 +117,14 @@
 
 
 def kernel(
-    load, labels, mask, table,
-    fwd, bwd, into_1, into_2, out_1, out_2, eigen_x, eigen_rows,
-    disp, resid,
-    modulus, faces, w, xs, xr, b1a, b1b, b2a, b2b, zb, fs, fr, zr, ys, yr, corr, rinv,
-    cys, cyr, czs, czr, cxs, cxr,
-    done, send_sem, recv_sem, out_sem,
+    load_in, labels_in, mask_in, table_in, *rest,
 ):
+    tables = rest[:TABLES]
+    (
+        disp, resid, modulus, faces, w, xs, xr, b1a, b1b, b2a, b2b, zb, fs, fr, zr, ys, yr, corr, rinv,
+        cys, cyr, czs, czr, cxs, cxr, send_sem, recv_sem, in_sem,
+        load, labels, mask, table, fwd, bwd, into_1, into_2, out_1, out_2, eigen_x, eigen_rows,
+    ) = rest[TABLES:]
     index = {a: lax.axis_index(a) for a in ("gx", "gy", "gz")}
     count = {a: lax.axis_size(a) for a in ("gx", "gy", "gz")}
     lower = {a: lax.rem(index[a] + count[a] - 1, count[a]) for a in index}
@@ -134,6 +136,15 @@
     for a in ("gx", "gy", "gz"):
         pl.semaphore_signal(barrier, inc=1, device_id={a: lower[a]}, device_id_type=MESH)
         pl.semaphore_signal(barrier, inc=1, device_id={a: upper[a]}, device_id_type=MESH)
+
+    sources = (load_in, labels_in, mask_in, table_in, *tables)
+    targets = (load, labels, mask, table, fwd, bwd, into_1, into_2, out_1, out_2, eigen_x, eigen_rows)
+    fetched = [
+        pltpu.make_async_copy(source, target, in_sem.at[number])
+        for number, (source, target) in enumerate(zip(sources, targets))
+    ]
+    for copy in fetched:
+        copy.start()
 
     def copies(slot, phase, down, up):
         a = AXIS[phase]
@@ -151,13 +162,13 @@
 
     def send(slot, phase, down, up):
         made = copies(slot, phase, down, up)
-        for copy in made:
-            copy.start()
+        for copy, there in zip(made, (has_lower, has_upper)):
+            pl.when(there[AXIS[phase]])(copy.start)
         pending[slot, phase] = made
 
     def arrive(slot, phase):
-        for copy in pending[slot, phase]:
-            copy.wait_recv()
+        for copy, there in zip(pending[slot, phase], (has_upper, has_lower)):
+            pl.when(there[AXIS[phase]])(copy.wait_recv)
 
     def flat(ref, slot):
         return ref.at[slot].reshape(PLANES * LENGTH, LANES)
@@ -393,15 +404,7 @@
             total = own
             for before in range(s):
                 total = corr[before * 3 + c] + total
-            done[0, c] = total
-            store(0, c, disp)
-
-    def store(which, c, target):
-        copy = pltpu.make_async_copy(done.at[which, c], target.at[c], out_sem.at[which * 3 + c])
-        copy.start()
-        stores.append(copy)
-
-    stores = []
+            disp[c] = total
 
     def update(s, c):
         slot = s * 3 + c
@@ -417,8 +420,7 @@
         for number, moved in enumerate(shifts(values, halo)):
             total = total + (ratio(c, number // 2) * 0.5) * faces[number] * (values - moved)
         if s == SWEEPS - 1:
-            done[1, c] = w[slot, 0:BRICK, 0:BRICK, :] - total
-            store(1, c, resid)
+            resid[c] = w[slot, 0:BRICK, 0:BRICK, :] - total
         else:
             w[slot + 3, 0:BRICK, 0:BRICK, :] = w[slot, 0:BRICK, 0:BRICK, :] - total
             a_pack(s + 1, c)
@@ -431,10 +433,14 @@
         for number, moved in enumerate(shifts(own, halo_get(6, low, high))):
             faces[number] = own + moved
 
+    fetched[0].wait()
     for c in range(3):
         a_pack(0, c)
     for slot in range(6):
         w[slot, LENGTH:] = jnp.zeros((PLANES - LENGTH, LENGTH, LANES), F32)
+
+    for copy in fetched[1:]:
+        copy.wait()
 
     def look(z, carry):
         picked = labels[z]
@@ -472,25 +478,23 @@
     for s, c, name in ORDER:
         stages[name](s, c)
 
-    for made in pending.values():
-        for copy in made:
-            copy.wait_send()
-    for copy in stores:
-        copy.wait()
+    for (_, phase), made in pending.items():
+        for copy, there in zip(made, (has_lower, has_upper)):
+            pl.when(there[AXIS[phase]])(copy.wait_send)
 
 
 def local(load, labels, mask, table):
     tables = constants()
     vmem = pl.BlockSpec(memory_space=pltpu.VMEM)
-    smem = pl.BlockSpec(memory_space=pltpu.SMEM)
+    hbm = pl.BlockSpec(memory_space=pltpu.HBM)
     slots = 3 * SWEEPS
     field = jax.ShapeDtypeStruct(load.shape, F32)
     block = (BRICK, BRICK, LANES)
     return pl.pallas_call(
         kernel,
         out_shape=(field, field),
-        in_specs=[vmem, vmem, vmem, smem] + [vmem] * len(tables),
-        out_specs=(pl.BlockSpec(memory_space=pl.ANY),) * 2,
+        in_specs=[hbm] * (4 + len(tables)),
+        out_specs=(vmem, vmem),
         scratch_shapes=[
             pltpu.VMEM(block, F32),
             pltpu.VMEM((6,) + block, F32),
@@ -515,15 +519,19 @@
             pltpu.VMEM((slots + 1, 2, BRICK, LANES), F32),
             pltpu.VMEM((slots + 1, 16, LANES), F32),
             pltpu.VMEM((slots + 1, 2, 16, LANES), F32),
-            pltpu.VMEM((2, 3) + block, F32),
             pltpu.SemaphoreType.DMA(((slots + 1) * PHASES * 2,)),
             pltpu.SemaphoreType.DMA(((slots + 1) * PHASES * 2,)),
-            pltpu.SemaphoreType.DMA((6,)),
+            pltpu.SemaphoreType.DMA((4 + len(tables),)),
+            pltpu.VMEM(load.shape, F32),
+            pltpu.VMEM(block, jnp.int32),
+            pltpu.VMEM(block, jnp.int32),
+            pltpu.SMEM(table.shape, F32),
+        ] + [pltpu.VMEM(t.shape, t.dtype) for t in tables] + [
         ],
         compiler_params=pltpu.CompilerParams(
-            collective_id=0, has_side_effects=True, vmem_limit_bytes=62 * 1024 * 1024
+            collective_id=0, has_side_effects=True, vmem_limit_bytes=44 * 1024 * 1024
         ),
-    )(load, labels, mask, table, *tables)
+    )(*(pltpu.with_memory_space_constraint(v, pltpu.HBM) for v in (load, labels, mask, table, *map(jnp.asarray, tables))))
 
 
 def solution(mesh):

time: 112 us -> 96.4 us (0.86)
  Pallas kernels: 107 us -> 93.4 us
  local copies, waits for them, and re-layouts: 3.93 us -> 2.29 us
    pallas_call x1, Pallas kernels: 107 us -> 93.4 us  [local(): pl.pallas_call(kernel, out_shape=(field, field), in_specs=[hbm] * (4 + le...]
    unnamed x4 -> x2, local copies, waits for them, and re-layouts: 3.93 us -> 2.29 us
where the time goes in v6:
time: 96.4 us; the launch traced here: 96.3 us
  Pallas kernels  93.4 us (97%)
  local copies, waits for them, and re-layouts  2.29 us (2%)
    pallas_call x1, Pallas kernels, local(): pl.pallas_call(kernel, out_shape=(field, field), in_specs=[hbm] * (4 + le...  93.4 us
    unnamed x2, local copies, waits for them, and re-layouts  2.29 us

profile of v6, /device:TPU:1, one launch (start us, length us, event | category | flops | bytes accessed | tf_op | source)
XLA Modules:
  0.0 96.3 jit_solution(2169019929173222262)
XLA Ops:
  0.6 93.4 %shard_map.131 = (f32[3,32,32,128]{3,2,1,0:T(8,128)S(1)}, f32[3,32,32,128]{3,2,1,0:T(8,128)S(1)}) custom-call(f32[3,32,32,128]{3,2,1,0:T(8,128)} %load_in.1, s32[32,32,128]{2,1,0:T(8,128)} %labels_in.1, s32[32,32,128]{2,1,0:T(8,128)} %mask_in.1, f32[16]{0:T(128)} %table_in.1, bf16[80,240]{1,0:T(8,128)(2,1)} %constant.16.clone.rest_0_, ...), custom_call_target="tpu_custom_call" | custom-call | tf_op jit(solution)/shard_map/pallas_call | solution.py:493
  94.0 1.1 %copy.16 = f32[3,32,32,128]{3,2,1,0:T(8,128)} copy(f32[3,32,32,128]{3,2,1,0:T(8,128)S(1)} %get-tuple-element.4) | data formatting | bytes 3145728
  95.1 1.1 %copy.17 = f32[3,32,32,128]{3,2,1,0:T(8,128)} copy(f32[3,32,32,128]{3,2,1,0:T(8,128)S(1)} %get-tuple-element.5) | data formatting | bytes 3145728

commit v7 on v6

--- a/solution.py
+++ b/solution.py
@@ -21,21 +21,22 @@
 REF_MODULUS = 1.5
 VOID_MODULUS = 0.1
 MESH = pl.DeviceIdType.MESH
-UNROLL = 5
+UNROLL = 10
+GROUPS = ((0, 4), (4, 8), (8, 13))
 PHASES = 10
 AY, AZ, AE, AX, BX, BZ, BY, CY, CZ, CX = range(PHASES)
 AXIS = ("gy", "gz", "gz", "gx", "gx", "gz", "gy", "gy", "gz", "gx")
 PLANES = 42
-TABLES = 8
+TABLES = 6
 ORDER = (
     (0, 0, "a_z"), (0, 1, "a_z"), (0, 0, "a_x"), (0, 2, "a_z"), (0, 1, "a_x"), (0, 0, "s1"), (0, 0, "s2"),
-    (0, 0, "s3"), (0, 1, "s1"), (0, 2, "a_x"), (0, 0, "stiff"), (0, 0, "b_z"), (0, 1, "s2"), (0, 1, "s3"),
-    (0, 0, "b_y"), (0, 2, "s1"), (0, 1, "b_z"), (0, 2, "s2"), (0, 2, "s3"), (0, 0, "c_start"), (0, 1, "b_y"),
-    (0, 2, "b_z"), (0, 0, "update"), (0, 1, "c_start"), (0, 2, "b_y"), (1, 0, "a_z"), (0, 1, "update"),
-    (1, 0, "a_x"), (0, 2, "c_start"), (1, 1, "a_z"), (0, 2, "update"), (1, 0, "s1"), (1, 1, "a_x"), (1, 0, "s2"),
+    (0, 0, "s3"), (0, 1, "s1"), (0, 2, "a_x"), (0, 1, "s2"), (0, 1, "s3"), (0, 0, "stiff"), (0, 0, "b_z"),
+    (0, 2, "s1"), (0, 2, "s2"), (0, 1, "b_z"), (0, 2, "s3"), (0, 0, "b_y"), (0, 2, "b_z"), (0, 1, "b_y"),
+    (0, 0, "c_start"), (0, 2, "b_y"), (0, 1, "c_start"), (0, 0, "update"), (0, 1, "update"), (1, 0, "a_z"),
+    (0, 2, "c_start"), (1, 1, "a_z"), (1, 0, "a_x"), (0, 2, "update"), (1, 1, "a_x"), (1, 0, "s1"), (1, 0, "s2"),
     (1, 0, "s3"), (1, 2, "a_z"), (1, 1, "s1"), (1, 1, "s2"), (1, 2, "a_x"), (1, 0, "b_z"), (1, 1, "s3"),
     (1, 2, "s1"), (1, 2, "s2"), (1, 1, "b_z"), (1, 2, "s3"), (1, 0, "b_y"), (1, 2, "b_z"), (1, 1, "b_y"),
-    (1, 2, "b_y"), (1, 0, "c_start"), (1, 1, "c_start"), (1, 2, "c_start"), (1, 0, "update"), (1, 1, "update"),
+    (1, 2, "b_y"), (1, 0, "c_start"), (1, 1, "c_start"), (1, 2, "c_start"), (1, 1, "update"), (1, 0, "update"),
     (1, 2, "update"),
 )
 F32 = jnp.float32
@@ -93,17 +94,15 @@
         return np.concatenate([high(both), high(both), low(both)], axis=1)
 
     def tall(*parts):
-        blank = np.zeros((2 * LANES - sum(p.shape[0] for p in parts), WIDE))
+        blank = np.zeros((4 * LANES - sum(p.shape[0] for p in parts), WIDE))
         return np.concatenate(parts + (blank,))
 
     head, tail = out[:LANES], out[LANES:LANES + rest]
     return [m.astype(BF16) for m in (
         pair(forward),
         pair(backward),
-        tall(high(into), high(into)),
-        tall(low(into), high(into_edge), high(into_edge), low(into_edge)),
-        tall(high(head), high(head)),
-        tall(low(head), high(tail), high(tail), low(tail)),
+        tall(high(into), high(into), low(into), high(into_edge), high(into_edge), low(into_edge)),
+        tall(high(head), high(head), low(head), high(tail), high(tail), low(tail)),
     )] + [eigen_x.astype(np.float32), np.ascontiguousarray(eigen_lanes).astype(np.float32)]
 
 
@@ -121,9 +120,9 @@
 ):
     tables = rest[:TABLES]
     (
-        disp, resid, modulus, faces, w, xs, xr, b1a, b1b, b2a, b2b, zb, fs, fr, zr, ys, yr, corr, rinv,
+        disp, resid, modulus, faces, centre, w, xs, xr, b1a, b1b, b2a, b2b, zb, fs, fr, zr, ys, yr, corr, rinv,
         cys, cyr, czs, czr, cxs, cxr, send_sem, recv_sem, in_sem,
-        load, labels, mask, table, fwd, bwd, into_1, into_2, out_1, out_2, eigen_x, eigen_rows,
+        load, labels, mask, table, fwd, bwd, into, out_of, eigen_x, eigen_rows,
     ) = rest[TABLES:]
     index = {a: lax.axis_index(a) for a in ("gx", "gy", "gz")}
     count = {a: lax.axis_size(a) for a in ("gx", "gy", "gz")}
@@ -138,7 +137,7 @@
         pl.semaphore_signal(barrier, inc=1, device_id={a: upper[a]}, device_id_type=MESH)
 
     sources = (load_in, labels_in, mask_in, table_in, *tables)
-    targets = (load, labels, mask, table, fwd, bwd, into_1, into_2, out_1, out_2, eigen_x, eigen_rows)
+    targets = (load, labels, mask, table, fwd, bwd, into, out_of, eigen_x, eigen_rows)
     fetched = [
         pltpu.make_async_copy(source, target, in_sem.at[number])
         for number, (source, target) in enumerate(zip(sources, targets))
@@ -313,16 +312,17 @@
             group = near[first:first + 5].reshape(-1, LANES)
             blank = jnp.zeros((LANES - group.shape[0], LANES), F32)
             sides.append(jnp.transpose(jnp.concatenate([group, blank], axis=0)))
-        for i in range(CHUNKS):
-            at = pl.ds(i * LANES, LANES)
-            side = sides[i // 5]
-            if i % 5:
-                side = pltpu.roll(side, LANES - 24 * (i % 5), 1)
-            high, low = halves(rows[at, :])
-            out = dot(jnp.concatenate([high, low], axis=1), into_1[...])
-            out += dot(jnp.concatenate([high, side.astype(BF16)], axis=1), into_2[...])
-            b1a[at, :] = out[:, :LANES]
-            b1b[at, :] = out[:, LANES:]
+        for first, last in GROUPS:
+            parts = []
+            for i in range(first, last):
+                side = sides[i // 5]
+                if i % 5:
+                    side = pltpu.roll(side, LANES - 24 * (i % 5), 1)
+                high, low = halves(rows[i * LANES:(i + 1) * LANES, :])
+                parts.append(jnp.concatenate([high, low, high, side.astype(BF16)], axis=1))
+            out = dot(jnp.concatenate(parts, axis=0), into[...])
+            b1a[first * LANES:last * LANES, :] = out[:, :LANES]
+            b1b[first * LANES:last * LANES, :] = out[:, LANES:]
 
         transform(fwd, one, two, True)
 
@@ -336,17 +336,20 @@
 
         rows = flat(zb, slot)
         margin = jnp.zeros((LANES, LANES), F32)
-        for i in range(CHUNKS):
-            at = pl.ds(i * LANES, LANES)
-            high, low = halves(b1a[at, :])
-            tail = b1b[at, :]
-            tail_high = tail.astype(BF16).astype(F32)
-            packed = tail_high + pltpu.roll(tail - tail_high, 32, 1) + pltpu.roll(tail_high, 64, 1)
-            out = dot(jnp.concatenate([high, low], axis=1), out_1[...])
-            out += dot(jnp.concatenate([high, packed.astype(BF16)], axis=1), out_2[...])
-            rows[at, :] = out[:, :LANES]
-            part = out[:, LANES:]
-            margin += pltpu.roll(part, 8 * i, 1) if i else part
+        for first, last in GROUPS:
+            parts = []
+            for i in range(first, last):
+                at = pl.ds(i * LANES, LANES)
+                high, low = halves(b1a[at, :])
+                tail = b1b[at, :]
+                tail_high = tail.astype(BF16).astype(F32)
+                packed = tail_high + pltpu.roll(tail - tail_high, 32, 1) + pltpu.roll(tail_high, 64, 1)
+                parts.append(jnp.concatenate([high, low, high, packed.astype(BF16)], axis=1))
+            out = dot(jnp.concatenate(parts, axis=0), out_of[...])
+            rows[first * LANES:last * LANES, :] = out[:, :LANES]
+            for i in range(first, last):
+                part = out[(i - first) * LANES:(i - first + 1) * LANES, LANES:]
+                margin += pltpu.roll(part, 8 * i, 1) if i else part
         margin = jnp.transpose(margin)[:CHUNKS * 8].reshape(CHUNKS, 8, LANES)
         fs[slot, 0] = margin[:, :MARGIN]
         fs[slot, 1] = margin[:, MARGIN:]
@@ -416,9 +419,11 @@
             keep(has_upper["gy"], cyr[slot, 1] + margins[:, MARGIN, :]),
         )
         values = corr[slot]
-        total = SIGMA_SHIFT * modulus[...] * values
-        for number, moved in enumerate(shifts(values, halo)):
-            total = total + (ratio(c, number // 2) * 0.5) * faces[number] * (values - moved)
+        total = centre[c] * values
+        moved = list(shifts(values, halo))
+        for k in range(3):
+            part = faces[2 * k] * moved[2 * k] + faces[2 * k + 1] * moved[2 * k + 1]
+            total = total - (part * ratio(c, k) if ratio(c, k) != 1.0 else part)
         if s == SWEEPS - 1:
             resid[c] = w[slot, 0:BRICK, 0:BRICK, :] - total
         else:
@@ -431,7 +436,13 @@
         own = modulus[...]
         low, high = keep(has_lower["gy"], cyr[6, 0]), keep(has_upper["gy"], cyr[6, 1])
         for number, moved in enumerate(shifts(own, halo_get(6, low, high))):
-            faces[number] = own + moved
+            faces[number] = 0.5 * (own + moved)
+        sums = [faces[2 * k] + faces[2 * k + 1] for k in range(3)]
+        for component in range(3):
+            total = SIGMA_SHIFT * own
+            for k in range(3):
+                total = total + ratio(component, k) * sums[k]
+            centre[component] = total
 
     fetched[0].wait()
     for c in range(3):
@@ -498,6 +509,7 @@
         scratch_shapes=[
             pltpu.VMEM(block, F32),
             pltpu.VMEM((6,) + block, F32),
+            pltpu.VMEM((3,) + block, F32),
             pltpu.VMEM((slots, PLANES, LENGTH, LANES), F32),
             pltpu.VMEM((slots, 2, CHUNKS, MARGIN, LANES), F32),
             pltpu.VMEM((slots, 2, CHUNKS, MARGIN, LANES), F32),

time: 96.4 us -> 93.9 us (0.974)
  Pallas kernels: 93.4 us -> 90.5 us
    pallas_call x1, Pallas kernels: 93.4 us -> 90.5 us  [local(): pl.pallas_call(kernel, out_shape=(field, field), in_specs=[hbm] * (4 + le...]
where the time goes in v7:
time: 93.9 us; the launch traced here: 93.5 us
  Pallas kernels  90.5 us (96%)
  local copies, waits for them, and re-layouts  2.29 us (2%)
    pallas_call x1, Pallas kernels, local(): pl.pallas_call(kernel, out_shape=(field, field), in_specs=[hbm] * (4 + le...  90.5 us
    unnamed x2, local copies, waits for them, and re-layouts  2.29 us

profile of v7, /device:TPU:1, one launch (start us, length us, event | category | flops | bytes accessed | tf_op | source)
XLA Modules:
  0.0 93.5 jit_solution(6015492193726386269)
XLA Ops:
  0.6 90.5 %shard_map.113 = (f32[3,32,32,128]{3,2,1,0:T(8,128)S(1)}, f32[3,32,32,128]{3,2,1,0:T(8,128)S(1)}) custom-call(f32[3,32,32,128]{3,2,1,0:T(8,128)} %load_in.1, s32[32,32,128]{2,1,0:T(8,128)} %labels_in.1, s32[32,32,128]{2,1,0:T(8,128)} %mask_in.1, f32[16]{0:T(128)} %table_in.1, bf16[80,240]{1,0:T(8,128)(2,1)} %constant.12.clone.rest_0_, ...), custom_call_target="tpu_custom_call" | custom-call | tf_op jit(solution)/shard_map/pallas_call | solution.py:504
  91.2 1.1 %copy.14 = f32[3,32,32,128]{3,2,1,0:T(8,128)} copy(f32[3,32,32,128]{3,2,1,0:T(8,128)S(1)} %get-tuple-element.4) | data formatting | bytes 3145728
  92.3 1.1 %copy.15 = f32[3,32,32,128]{3,2,1,0:T(8,128)} copy(f32[3,32,32,128]{3,2,1,0:T(8,128)S(1)} %get-tuple-element.5) | data formatting | bytes 3145728

commit v8 on v7

--- a/solution.py
+++ b/solution.py
@@ -30,12 +30,12 @@
 TABLES = 6
 ORDER = (
     (0, 0, "a_z"), (0, 1, "a_z"), (0, 0, "a_x"), (0, 2, "a_z"), (0, 1, "a_x"), (0, 0, "s1"), (0, 0, "s2"),
-    (0, 0, "s3"), (0, 1, "s1"), (0, 2, "a_x"), (0, 1, "s2"), (0, 1, "s3"), (0, 0, "stiff"), (0, 0, "b_z"),
-    (0, 2, "s1"), (0, 2, "s2"), (0, 1, "b_z"), (0, 2, "s3"), (0, 0, "b_y"), (0, 2, "b_z"), (0, 1, "b_y"),
-    (0, 0, "c_start"), (0, 2, "b_y"), (0, 1, "c_start"), (0, 0, "update"), (0, 1, "update"), (1, 0, "a_z"),
-    (0, 2, "c_start"), (1, 1, "a_z"), (1, 0, "a_x"), (0, 2, "update"), (1, 1, "a_x"), (1, 0, "s1"), (1, 0, "s2"),
+    (0, 0, "s3"), (0, 2, "a_x"), (0, 1, "s1"), (0, 0, "b_z"), (0, 1, "s2"), (0, 1, "s3"), (0, 0, "b_y"),
+    (0, 2, "s1"), (0, 1, "b_z"), (0, 2, "s2"), (0, 2, "s3"), (0, 0, "c_start"), (0, 1, "b_y"), (0, 0, "stiff"),
+    (0, 2, "b_z"), (0, 0, "update"), (0, 1, "c_start"), (0, 2, "b_y"), (0, 1, "update"), (1, 0, "a_z"),
+    (0, 2, "c_start"), (1, 0, "a_x"), (1, 1, "a_z"), (0, 2, "update"), (1, 0, "s1"), (1, 1, "a_x"), (1, 0, "s2"),
     (1, 0, "s3"), (1, 2, "a_z"), (1, 1, "s1"), (1, 1, "s2"), (1, 2, "a_x"), (1, 0, "b_z"), (1, 1, "s3"),
-    (1, 2, "s1"), (1, 2, "s2"), (1, 1, "b_z"), (1, 2, "s3"), (1, 0, "b_y"), (1, 2, "b_z"), (1, 1, "b_y"),
+    (1, 2, "s1"), (1, 2, "s2"), (1, 1, "b_z"), (1, 2, "s3"), (1, 0, "b_y"), (1, 1, "b_y"), (1, 2, "b_z"),
     (1, 2, "b_y"), (1, 0, "c_start"), (1, 1, "c_start"), (1, 2, "c_start"), (1, 1, "update"), (1, 0, "update"),
     (1, 2, "update"),
 )
@@ -136,8 +136,8 @@
         pl.semaphore_signal(barrier, inc=1, device_id={a: lower[a]}, device_id_type=MESH)
         pl.semaphore_signal(barrier, inc=1, device_id={a: upper[a]}, device_id_type=MESH)
 
-    sources = (load_in, labels_in, mask_in, table_in, *tables)
-    targets = (load, labels, mask, table, fwd, bwd, into, out_of, eigen_x, eigen_rows)
+    sources = (*(load_in.at[c] for c in range(3)), labels_in, mask_in, table_in, *tables)
+    targets = (*(load.at[c] for c in range(3)), labels, mask, table, fwd, bwd, into, out_of, eigen_x, eigen_rows)
     fetched = [
         pltpu.make_async_copy(source, target, in_sem.at[number])
         for number, (source, target) in enumerate(zip(sources, targets))
@@ -444,13 +444,16 @@
                 total = total + ratio(component, k) * sums[k]
             centre[component] = total
 
-    fetched[0].wait()
     for c in range(3):
+        fetched[c].wait()
         a_pack(0, c)
+        if c == 0:
+            pl.semaphore_wait(barrier, 6)
+        a_send(0, c)
     for slot in range(6):
         w[slot, LENGTH:] = jnp.zeros((PLANES - LENGTH, LENGTH, LANES), F32)
 
-    for copy in fetched[1:]:
+    for copy in fetched[3:]:
         copy.wait()
 
     def look(z, carry):
@@ -464,6 +467,8 @@
     lax.fori_loop(0, BRICK, look, 0)
     y_pack(6, modulus[...])
     xz_pack(6, modulus[...])
+    y_send(6)
+    xz_send(6)
 
     for c in range(3):
         def invert(y, carry, c=c):
@@ -477,12 +482,6 @@
             return carry
 
         lax.fori_loop(0, LENGTH, invert, 0)
-
-    pl.semaphore_wait(barrier, 6)
-    for c in range(3):
-        a_send(0, c)
-    y_send(6)
-    xz_send(6)
 
     stages = dict(a_z=a_z, a_x=a_x, s1=s1, s2=s2, s3=s3, b_z=b_z, b_y=b_y, c_start=c_start, update=update,
                   stiff=stiff)
@@ -533,7 +532,7 @@
             pltpu.VMEM((slots + 1, 2, 16, LANES), F32),
             pltpu.SemaphoreType.DMA(((slots + 1) * PHASES * 2,)),
             pltpu.SemaphoreType.DMA(((slots + 1) * PHASES * 2,)),
-            pltpu.SemaphoreType.DMA((4 + len(tables),)),
+            pltpu.SemaphoreType.DMA((6 + len(tables),)),
             pltpu.VMEM(load.shape, F32),
             pltpu.VMEM(block, jnp.int32),
             pltpu.VMEM(block, jnp.int32),

time: 93.9 us -> 88.6 us (0.944)
  Pallas kernels: 90.5 us -> 84.9 us
    pallas_call x1, Pallas kernels: 90.5 us -> 84.9 us  [local(): pl.pallas_call(kernel, out_shape=(field, field), in_specs=[hbm] * (4 + le...]
where the time goes in v8:
time: 88.6 us; the launch traced here: 87.8 us
  Pallas kernels  84.9 us (96%)
  local copies, waits for them, and re-layouts  2.29 us (3%)
    pallas_call x1, Pallas kernels, local(): pl.pallas_call(kernel, out_shape=(field, field), in_specs=[hbm] * (4 + le...  84.9 us
    unnamed x2, local copies, waits for them, and re-layouts  2.29 us

profile of v8, /device:TPU:1, one launch (start us, length us, event | category | flops | bytes accessed | tf_op | source)
XLA Modules:
  0.0 87.8 jit_solution(15856440794049762378)
XLA Ops:
  0.6 84.9 %shard_map.113 = (f32[3,32,32,128]{3,2,1,0:T(8,128)S(1)}, f32[3,32,32,128]{3,2,1,0:T(8,128)S(1)}) custom-call(f32[3,32,32,128]{3,2,1,0:T(8,128)} %load_in.1, s32[32,32,128]{2,1,0:T(8,128)} %labels_in.1, s32[32,32,128]{2,1,0:T(8,128)} %mask_in.1, f32[16]{0:T(128)} %table_in.1, bf16[80,240]{1,0:T(8,128)(2,1)} %constant.12.clone.rest_0_, ...), custom_call_target="tpu_custom_call" | custom-call | tf_op jit(solution)/shard_map/pallas_call | solution.py:503
  85.5 1.1 %copy.14 = f32[3,32,32,128]{3,2,1,0:T(8,128)} copy(f32[3,32,32,128]{3,2,1,0:T(8,128)S(1)} %get-tuple-element.4) | data formatting | bytes 3145728
  86.7 1.1 %copy.15 = f32[3,32,32,128]{3,2,1,0:T(8,128)} copy(f32[3,32,32,128]{3,2,1,0:T(8,128)S(1)} %get-tuple-element.5) | data formatting | bytes 3145728

commit v9 on v8

--- a/solution.py
+++ b/solution.py
@@ -31,12 +31,12 @@
 ORDER = (
     (0, 0, "a_z"), (0, 1, "a_z"), (0, 0, "a_x"), (0, 2, "a_z"), (0, 1, "a_x"), (0, 0, "s1"), (0, 0, "s2"),
     (0, 0, "s3"), (0, 2, "a_x"), (0, 1, "s1"), (0, 0, "b_z"), (0, 1, "s2"), (0, 1, "s3"), (0, 0, "b_y"),
-    (0, 2, "s1"), (0, 1, "b_z"), (0, 2, "s2"), (0, 2, "s3"), (0, 0, "c_start"), (0, 1, "b_y"), (0, 0, "stiff"),
-    (0, 2, "b_z"), (0, 0, "update"), (0, 1, "c_start"), (0, 2, "b_y"), (0, 1, "update"), (1, 0, "a_z"),
+    (0, 0, "stiff"), (0, 2, "s1"), (0, 1, "b_z"), (0, 2, "s2"), (0, 2, "s3"), (0, 0, "c_start"), (0, 1, "b_y"),
+    (0, 2, "b_z"), (0, 0, "update"), (0, 1, "c_start"), (0, 2, "b_y"), (1, 0, "a_z"), (0, 1, "update"),
     (0, 2, "c_start"), (1, 0, "a_x"), (1, 1, "a_z"), (0, 2, "update"), (1, 0, "s1"), (1, 1, "a_x"), (1, 0, "s2"),
     (1, 0, "s3"), (1, 2, "a_z"), (1, 1, "s1"), (1, 1, "s2"), (1, 2, "a_x"), (1, 0, "b_z"), (1, 1, "s3"),
-    (1, 2, "s1"), (1, 2, "s2"), (1, 1, "b_z"), (1, 2, "s3"), (1, 0, "b_y"), (1, 1, "b_y"), (1, 2, "b_z"),
-    (1, 2, "b_y"), (1, 0, "c_start"), (1, 1, "c_start"), (1, 2, "c_start"), (1, 1, "update"), (1, 0, "update"),
+    (1, 2, "s1"), (1, 0, "b_y"), (1, 2, "s2"), (1, 1, "b_z"), (1, 2, "s3"), (1, 1, "b_y"), (1, 2, "b_z"),
+    (1, 0, "c_start"), (1, 2, "b_y"), (1, 1, "c_start"), (1, 0, "update"), (1, 2, "c_start"), (1, 1, "update"),
     (1, 2, "update"),
 )
 F32 = jnp.float32
@@ -364,15 +364,20 @@
         side = jnp.transpose(jnp.concatenate([near.reshape(CHUNKS * 8, LANES), blank], axis=0))
         rows = flat(zb, slot)
         edge = (lanes < MARGIN) | (lanes >= LANES - MARGIN)
-        for i in range(CHUNKS):
-            at = pl.ds(i * LANES, LANES)
-            rows[at, :] += jnp.where(edge, pltpu.roll(side, LANES - 8 * i - MARGIN, 1), 0.0)
-
+
+        def add(first, last):
+            for i in range(first, last):
+                at = pl.ds(i * LANES, LANES)
+                rows[at, :] += jnp.where(edge, pltpu.roll(side, LANES - 8 * i - MARGIN, 1), 0.0)
+
+        whole = OWNED // LANES
+        add(whole, CHUNKS)
         send(
             slot, BZ,
             (zb.at[slot, pl.ds(BRICK, MARGIN)], zr.at[slot, 1]),
             (zb.at[slot, pl.ds(BRICK + MARGIN, MARGIN)], zr.at[slot, 0]),
         )
+        add(0, whole)
 
     def b_y(s, c):
         slot = s * 3 + c

time: 88.6 us -> 89.1 us (level)
  no operation moved by 1% of the time
where the time goes in v9:
time: 89.1 us; the launch traced here: 87.6 us
  Pallas kernels  84.7 us (95%)
  local copies, waits for them, and re-layouts  2.29 us (3%)
    pallas_call x1, Pallas kernels, local(): pl.pallas_call(kernel, out_shape=(field, field), in_specs=[hbm] * (4 + le...  84.7 us
    unnamed x2, local copies, waits for them, and re-layouts  2.29 us

profile of v9, /device:TPU:1, one launch (start us, length us, event | category | flops | bytes accessed | tf_op | source)
XLA Modules:
  0.0 87.6 jit_solution(10278219434257471651)
XLA Ops:
  0.6 84.7 %shard_map.113 = (f32[3,32,32,128]{3,2,1,0:T(8,128)S(1)}, f32[3,32,32,128]{3,2,1,0:T(8,128)S(1)}) custom-call(f32[3,32,32,128]{3,2,1,0:T(8,128)} %load_in.1, s32[32,32,128]{2,1,0:T(8,128)} %labels_in.1, s32[32,32,128]{2,1,0:T(8,128)} %mask_in.1, f32[16]{0:T(128)} %table_in.1, bf16[80,240]{1,0:T(8,128)(2,1)} %constant.12.clone.rest_0_, ...), custom_call_target="tpu_custom_call" | custom-call | tf_op jit(solution)/shard_map/pallas_call | solution.py:508
  85.3 1.1 %copy.14 = f32[3,32,32,128]{3,2,1,0:T(8,128)} copy(f32[3,32,32,128]{3,2,1,0:T(8,128)S(1)} %get-tuple-element.4) | data formatting | bytes 3145728
  86.5 1.1 %copy.15 = f32[3,32,32,128]{3,2,1,0:T(8,128)} copy(f32[3,32,32,128]{3,2,1,0:T(8,128)S(1)} %get-tuple-element.5) | data formatting | bytes 3145728

commit v10 on v9

--- a/solution.py
+++ b/solution.py
@@ -21,7 +21,7 @@
 REF_MODULUS = 1.5
 VOID_MODULUS = 0.1
 MESH = pl.DeviceIdType.MESH
-UNROLL = 10
+UNROLL = 20
 GROUPS = ((0, 4), (4, 8), (8, 13))
 PHASES = 10
 AY, AZ, AE, AX, BX, BZ, BY, CY, CZ, CX = range(PHASES)
@@ -31,12 +31,12 @@
 ORDER = (
     (0, 0, "a_z"), (0, 1, "a_z"), (0, 0, "a_x"), (0, 2, "a_z"), (0, 1, "a_x"), (0, 0, "s1"), (0, 0, "s2"),
     (0, 0, "s3"), (0, 2, "a_x"), (0, 1, "s1"), (0, 0, "b_z"), (0, 1, "s2"), (0, 1, "s3"), (0, 0, "b_y"),
-    (0, 0, "stiff"), (0, 2, "s1"), (0, 1, "b_z"), (0, 2, "s2"), (0, 2, "s3"), (0, 0, "c_start"), (0, 1, "b_y"),
-    (0, 2, "b_z"), (0, 0, "update"), (0, 1, "c_start"), (0, 2, "b_y"), (1, 0, "a_z"), (0, 1, "update"),
+    (0, 2, "s1"), (0, 1, "b_z"), (0, 2, "s2"), (0, 2, "s3"), (0, 0, "c_start"), (0, 1, "b_y"), (0, 0, "stiff"),
+    (0, 2, "b_z"), (0, 0, "update"), (0, 1, "c_start"), (0, 2, "b_y"), (0, 1, "update"), (1, 0, "a_z"),
     (0, 2, "c_start"), (1, 0, "a_x"), (1, 1, "a_z"), (0, 2, "update"), (1, 0, "s1"), (1, 1, "a_x"), (1, 0, "s2"),
     (1, 0, "s3"), (1, 2, "a_z"), (1, 1, "s1"), (1, 1, "s2"), (1, 2, "a_x"), (1, 0, "b_z"), (1, 1, "s3"),
-    (1, 2, "s1"), (1, 0, "b_y"), (1, 2, "s2"), (1, 1, "b_z"), (1, 2, "s3"), (1, 1, "b_y"), (1, 2, "b_z"),
-    (1, 0, "c_start"), (1, 2, "b_y"), (1, 1, "c_start"), (1, 0, "update"), (1, 2, "c_start"), (1, 1, "update"),
+    (1, 2, "s1"), (1, 2, "s2"), (1, 1, "b_z"), (1, 2, "s3"), (1, 0, "b_y"), (1, 1, "b_y"), (1, 2, "b_z"),
+    (1, 2, "b_y"), (1, 0, "c_start"), (1, 1, "c_start"), (1, 2, "c_start"), (1, 1, "update"), (1, 0, "update"),
     (1, 2, "update"),
 )
 F32 = jnp.float32

time: 89.1 us -> 85.5 us (0.960)
  Pallas kernels: 84.7 us -> 81.7 us
    pallas_call x1, Pallas kernels: 84.7 us -> 81.7 us  [local(): pl.pallas_call(kernel, out_shape=(field, field), in_specs=[hbm] * (4 + le...]
where the time goes in v10:
time: 85.5 us; the launch traced here: 84.6 us
  Pallas kernels  81.7 us (96%)
  local copies, waits for them, and re-layouts  2.29 us (3%)
    pallas_call x1, Pallas kernels, local(): pl.pallas_call(kernel, out_shape=(field, field), in_specs=[hbm] * (4 + le...  81.7 us
    unnamed x2, local copies, waits for them, and re-layouts  2.29 us

profile of v10, /device:TPU:1, one launch (start us, length us, event | category | flops | bytes accessed | tf_op | source)
XLA Modules:
  0.0 84.6 jit_solution(13644980643305447260)
XLA Ops:
  0.6 81.7 %shard_map.113 = (f32[3,32,32,128]{3,2,1,0:T(8,128)S(1)}, f32[3,32,32,128]{3,2,1,0:T(8,128)S(1)}) custom-call(f32[3,32,32,128]{3,2,1,0:T(8,128)} %load_in.1, s32[32,32,128]{2,1,0:T(8,128)} %labels_in.1, s32[32,32,128]{2,1,0:T(8,128)} %mask_in.1, f32[16]{0:T(128)} %table_in.1, bf16[80,240]{1,0:T(8,128)(2,1)} %constant.12.clone.rest_0_, ...), custom_call_target="tpu_custom_call" | custom-call | tf_op jit(solution)/shard_map/pallas_call | solution.py:508
  82.3 1.1 %copy.14 = f32[3,32,32,128]{3,2,1,0:T(8,128)} copy(f32[3,32,32,128]{3,2,1,0:T(8,128)S(1)} %get-tuple-element.4) | data formatting | bytes 3145728
  83.4 1.1 %copy.15 = f32[3,32,32,128]{3,2,1,0:T(8,128)} copy(f32[3,32,32,128]{3,2,1,0:T(8,128)S(1)} %get-tuple-element.5) | data formatting | bytes 3145728
